TPU v7x, 32 devices: a whole 2x2x4 slice. The times are simulated.
32 devices in a mesh: groups: 2 (over y), sample: 4 (over z), tensor: 4 (over x, core).
Axes of the slice: x: 2, y: 2, z: 4, core: 2. Of those that a mesh axis runs over, the one named last changes fastest.
Arguments:
- queries: bfloat16 [4, 128, 8192], P(None, ('groups', 'sample'), 'tensor'), parts along dimension 1, may hold values from -8 to 8
- new_kv: bfloat16 [4, 128, 2048], P(None, ('groups', 'sample'), 'tensor'), parts along dimension 1, may hold values from -5 to 5
- gen_kv: bfloat16 [128, 512, 2048], P(('groups', 'sample'), None, 'tensor'), parts along dimension 0, may hold values from -5 to 5
- prefix_kv: bfloat16 [8, 256, 2048], P(('groups', 'sample'), None, 'tensor'), parts along dimension 0, may hold values from -5 to 5
- slot_prompt: int32 [8], P(('groups', 'sample')), parts along dimension 0, may hold values from 0 to 3, each once
- prefix_blocks: int32 [8], P(('groups', 'sample')), parts along dimension 0, may hold values from 1 to 2, as said below
- gen_len: int32 [128], P(('groups', 'sample')), parts along dimension 0, may hold values from 1 to 512, as said below
- out_weight: bfloat16 [8192, 4096], P('tensor', 'sample'), may hold values from -0.75 to 0.75
Outputs:
- mixed: bfloat16 [4, 128, 4096], P(None, ('groups', 'sample'), 'tensor'), parts along dimension 1
There are 2 independent parts, one for each index of `groups`. A program takes and returns all parts, laid end to end along the dimension named above; an argument that names none is the same for every part. Nothing has to cross between parts.
Inputs may be any that keep to these rules, and one draw needn't show every extreme that they name: `slot_prompt`: each slot holds one prompt's prefix and every prompt has a slot. `prefix_blocks`: some slot has 2 valid blocks. `gen_len`: some sequence has generated 512 tokens.
All inputs are finite; a program needn't handle non-finite values.
Results may differ from a plain program's by a relative error of at most 0.0057.
Values may be sent and summed in bfloat16 or wider, within the bound.
No kernel may reach another device: no remote copies, remote signals or barrier semaphores. Data moves between devices by JAX's collectives and lax.ppermute only.
A program may use at most 128 MiB of HBM per device.

v0:
```python
import functools

import jax
import jax.numpy as jnp
from jax import lax
from jax.experimental import pallas as pl
from jax.experimental.pallas import tpu as pltpu
from jax.sharding import PartitionSpec as P


HD = 128
BLOCK = 128
LOW = -1e30
EXTRA = 8


def nt(a, b):
    return lax.dot_general(a, b, (((1,), (1,)), ((), ())), preferred_element_type=jnp.float32)


def nn(a, b):
    return lax.dot_general(a, b, (((1,), (0,)), ((), ())), preferred_element_type=jnp.float32)


def in_hbm(x):
    return pltpu.with_memory_space_constraint(x, pltpu.HBM)


def payload_kernel(prompt_ref, blocks_ref, pre_ref, out_ref, sem):
    keys, kvw = pre_ref.shape[1:]
    copy = pltpu.make_async_copy(pre_ref, out_ref.at[:, pl.ds(0, keys), :], sem)
    copy.start()
    shape = (1, out_ref.shape[1] - keys, kvw // 2)
    out_ref[:, keys:, : kvw // 2] = jnp.full(shape, prompt_ref[0], jnp.float32).astype(jnp.bfloat16)
    out_ref[:, keys:, kvw // 2 :] = jnp.full(shape, blocks_ref[0], jnp.float32).astype(jnp.bfloat16)
    copy.wait()


def make_payload(prefix_kv, slot_prompt, prefix_blocks):
    _, keys, kvw = prefix_kv.shape
    smem = pl.BlockSpec(memory_space=pltpu.SMEM)
    return pl.pallas_call(
        payload_kernel,
        out_shape=jax.ShapeDtypeStruct((1, keys + EXTRA, kvw), prefix_kv.dtype),
        in_specs=[smem, smem, pl.BlockSpec(memory_space=pl.ANY)],
        out_specs=pl.BlockSpec(memory_space=pltpu.VMEM),
        scratch_shapes=[pltpu.SemaphoreType.DMA],
        compiler_params=pltpu.CompilerParams(vmem_limit_bytes=4 << 20),
        name="make_payload",
    )(slot_prompt, prefix_blocks, in_hbm(prefix_kv))


def gen_rows(steps, group, row, len_ref, q_ref, new_ref, kv_ref, acc_ref, ml_ref, q_at):
    batch, keys, kvw = kv_ref.shape
    heads = kvw // (2 * HD)
    span = steps * group
    rows = new_ref.shape[1]
    scale = HD ** (-0.5)
    col = lax.broadcasted_iota(jnp.int32, (span, keys), 1)
    new_col = lax.broadcasted_iota(jnp.int32, (span, steps * rows), 1)
    new_row, new_step = new_col % rows, new_col // rows
    step_of = lax.broadcasted_iota(jnp.int32, (span, steps * rows), 0) // group
    causal = new_step <= step_of
    lane = lax.broadcasted_iota(jnp.int32, (span, HD), 1)
    for h in range(heads):
        base = h * 2 * HD
        at = slice(h * span, (h + 1) * span)
        fresh = new_ref[:, :, base : base + 2 * HD].reshape(steps * rows, 2 * HD)
        qs = [q_ref[q_at + b, at, :] for b in range(batch)]
        scores = [nt(qs[b], kv_ref[b, :, base : base + HD]) for b in range(batch)]
        news = nt(jnp.concatenate(qs, axis=0), fresh[:, :HD])
        exps, new_exps = [], []
        for b in range(batch):
            s = jnp.where(col < len_ref[row + b], scores[b] * scale, LOW)
            n = news[b * span : (b + 1) * span] * scale
            n = jnp.where(causal & (new_row == row + b), n, LOW)
            top = jnp.maximum(
                jnp.max(s, axis=1, keepdims=True), jnp.max(n, axis=1, keepdims=True)
            )
            e, f = jnp.exp(s - top), jnp.exp(n - top)
            total = jnp.sum(e, axis=1, keepdims=True) + jnp.sum(f, axis=1, keepdims=True)
            ml_ref[b, at, :] = jnp.where(lane < HD // 2, top, total)
            exps.append(e.astype(jnp.bfloat16))
            new_exps.append(f.astype(jnp.bfloat16))
        more = nn(jnp.concatenate(new_exps, axis=0), fresh[:, HD:])
        for b in range(batch):
            acc = nn(exps[b], kv_ref[b, :, base + HD : base + 2 * HD])
            acc_ref[b, at, :] = acc + more[b * span : (b + 1) * span]


def gen_kernel(
    steps,
    heads,
    group,
    len_ref,
    q_ref,
    new_ref,
    kv_ref,
    grouped_ref,
    acc_ref,
    ml_ref,
    scr,
):
    rows = q_ref.shape[1]
    span = steps * group
    per_row = heads * span
    batch = kv_ref.shape[0]

    @pl.when(pl.program_id(0) == 0)
    def _():
        for s in range(steps):
            for hg in range(heads * group):
                tile = q_ref[s, :, hg * HD : (hg + 1) * HD].astype(jnp.float32)
                start = (hg // group) * span + s * group + hg % group
                scr[pl.ds(start, rows, stride=per_row), :] = tile
        for r in range(rows):
            grouped_ref[r] = scr[r * per_row : (r + 1) * per_row, :].astype(jnp.bfloat16)

    row = pl.program_id(0) * batch
    gen_rows(steps, group, row, len_ref, grouped_ref, new_ref, kv_ref, acc_ref, ml_ref, row)


def gen_attention(queries, fresh, cached, lengths, heads, batch):
    steps, rows, width = queries.shape
    keys, kvw = cached.shape[1:]
    group = width // (heads * HD)
    per_row = heads * steps * group
    sums = jax.ShapeDtypeStruct((rows, per_row, HD), jnp.float32)
    sum_spec = pl.BlockSpec((batch, per_row, HD), lambda r, n: (r, 0, 0))
    return pl.pallas_call(
        functools.partial(gen_kernel, steps, heads, group),
        out_shape=(
            jax.ShapeDtypeStruct((rows, per_row, HD), jnp.bfloat16),
            sums,
            sums,
        ),
        grid_spec=pltpu.PrefetchScalarGridSpec(
            num_scalar_prefetch=1,
            grid=(rows // batch,),
            in_specs=[
                pl.BlockSpec((steps, rows, width), lambda r, n: (0, 0, 0)),
                pl.BlockSpec((steps, rows, kvw), lambda r, n: (0, 0, 0)),
                pl.BlockSpec((batch, keys, kvw), lambda r, n: (r, 0, 0)),
            ],
            out_specs=[
                pl.BlockSpec((rows, per_row, HD), lambda r, n: (0, 0, 0)),
                sum_spec,
                sum_spec,
            ],
            scratch_shapes=[pltpu.VMEM((rows * per_row, HD), jnp.float32)],
        ),
        compiler_params=pltpu.CompilerParams(vmem_limit_bytes=16 << 20),
        cost_estimate=pl.CostEstimate(
            flops=4 * rows * per_row * keys * HD,
            bytes_accessed=2 * rows * keys * kvw,
            transcendentals=rows * per_row * keys,
        ),
        name="gen_attention",
    )(lengths, in_hbm(queries), in_hbm(fresh), in_hbm(cached))


def add_slots_kernel(slots, steps, group, count, *refs):
    pre_refs, (q_ref, acc_ref, ml_ref, out_ref, scr) = refs[:count], refs[count:]
    rows = q_ref.shape[0]
    keys = pre_refs[0].shape[1] - EXTRA
    kvw = pre_refs[0].shape[2]
    heads = kvw // (2 * HD)
    span = steps * group
    members = rows // slots
    order = range(members)
    tall = members * span
    scale = HD ** (-0.5)
    col = lax.broadcasted_iota(jnp.int32, (tall, keys), 1)
    for n, pre_ref in enumerate(pre_refs):
        extra = pre_ref[0, keys:, :].astype(jnp.float32)
        prompt = jnp.max(extra[:, :HD]).astype(jnp.int32)
        length = jnp.max(extra[:, kvw // 2 : kvw // 2 + HD]).astype(jnp.int32) * BLOCK
        for h in range(heads):
            base = h * 2 * HD
            at = slice(h * span, (h + 1) * span)
            q = jnp.concatenate([q_ref[prompt + i * slots, at, :] for i in order], axis=0)
            ml = jnp.concatenate([ml_ref[prompt + i * slots, at, :] for i in order], axis=0)
            acc = jnp.concatenate([acc_ref[prompt + i * slots, at, :] for i in order], axis=0)
            s = nt(q, pre_ref[0, :keys, base : base + HD]) * scale
            s = jnp.where(col < length, s, LOW)
            old_top = ml[:, 0:1]
            old_total = ml[:, HD // 2 : HD // 2 + 1]
            top = jnp.maximum(old_top, jnp.max(s, axis=1, keepdims=True))
            e = jnp.exp(s - top)
            carry = jnp.exp(old_top - top)
            total = jnp.sum(e, axis=1, keepdims=True) + carry * old_total
            add = nn(e.astype(jnp.bfloat16), pre_ref[0, :keys, base + HD : base + 2 * HD])
            scr[(n * heads + h) * tall : (n * heads + h + 1) * tall, :] = (add + carry * acc) / total
    tile_rows = members * steps
    for n in range(count):
        for h in range(heads):
            for g in range(group):
                tile = scr[pl.ds((n * heads + h) * tall + g, tile_rows, stride=group), :]
                cols = slice((h * group + g) * HD, (h * group + g + 1) * HD)
                out_ref[n * tile_rows : (n + 1) * tile_rows, cols] = tile.astype(jnp.bfloat16)


def add_slots(grouped, acc, ml, payloads, slots, steps, heads):
    rows, per_row, _ = grouped.shape
    group = per_row // (heads * steps)
    count = len(payloads)
    keys, kvw = payloads[0].shape[1:]
    vmem = pl.BlockSpec(memory_space=pltpu.VMEM)
    shape = (count * rows // slots * steps, heads * group * HD)
    return pl.pallas_call(
        functools.partial(add_slots_kernel, slots, steps, group, count),
        out_shape=jax.ShapeDtypeStruct(shape, jnp.bfloat16),
        in_specs=[vmem] * (count + 3),
        out_specs=vmem,
        scratch_shapes=[pltpu.VMEM((count * rows // slots * per_row, HD), jnp.float32)],
        compiler_params=pltpu.CompilerParams(vmem_limit_bytes=8 << 20),
        cost_estimate=pl.CostEstimate(
            flops=4 * count * rows * per_row * keys * HD // slots,
            bytes_accessed=2 * count * keys * kvw,
            transcendentals=count * rows * per_row * keys // slots,
        ),
    )(*payloads, grouped, acc, ml)


def order_kernel(steps, rows, *refs):
    pre_refs, out_ref = refs[:-1], refs[-1]
    slots = len(pre_refs)
    size = out_ref.shape[0]
    group = size // slots
    place = lax.broadcasted_iota(jnp.int32, (size, size), 0)
    came = lax.broadcasted_iota(jnp.int32, (size, size), 1)
    prompt = jnp.zeros((size, size), jnp.int32)
    for k, pre_ref in enumerate(pre_refs):
        extra = pre_ref[0, pre_ref.shape[1] - EXTRA :, :HD].astype(jnp.float32)
        prompt = jnp.where(came // group == k, jnp.max(extra).astype(jnp.int32), prompt)
    row = prompt + came % group // steps * slots
    hit = place == came % steps * rows + row
    out_ref[...] = jnp.where(hit, 1.0, 0.0).astype(jnp.bfloat16)


def row_order(payloads, steps, rows):
    vmem = pl.BlockSpec(memory_space=pltpu.VMEM)
    return pl.pallas_call(
        functools.partial(order_kernel, steps, rows),
        out_shape=jax.ShapeDtypeStruct((steps * rows, steps * rows), jnp.bfloat16),
        in_specs=[vmem] * len(payloads),
        out_specs=vmem,
        compiler_params=pltpu.CompilerParams(vmem_limit_bytes=4 << 20),
        name="row_order",
    )(*payloads)


def finish_kernel(order_ref, a_ref, b_ref, out_ref):
    total = a_ref[...].astype(jnp.float32) + b_ref[...].astype(jnp.float32)
    out_ref[...] = nn(order_ref[...], total.astype(jnp.bfloat16)).astype(jnp.bfloat16)


def finish(order, a, b):
    vmem = pl.BlockSpec(memory_space=pltpu.VMEM)
    return pl.pallas_call(
        finish_kernel,
        out_shape=jax.ShapeDtypeStruct(a.shape, jnp.bfloat16),
        in_specs=[vmem] * 3,
        out_specs=vmem,
        compiler_params=pltpu.CompilerParams(vmem_limit_bytes=4 << 20),
        name="finish",
    )(order, a, b)


def hold_kernel(w_ref, out_ref, sems):
    rows = w_ref.shape[0] // sems.shape[0]
    copies = []
    for c in range(sems.shape[0]):
        at = pl.ds(c * rows, rows)
        copies.append(pltpu.make_async_copy(w_ref.at[at], out_ref.at[at], sems.at[c]))
        copies[c].start()
    for copy in copies:
        copy.wait()


def hold(weight):
    return pl.pallas_call(
        hold_kernel,
        out_shape=jax.ShapeDtypeStruct(weight.shape, weight.dtype),
        in_specs=[pl.BlockSpec(memory_space=pl.ANY)],
        out_specs=pl.BlockSpec(memory_space=pltpu.VMEM),
        scratch_shapes=[pltpu.SemaphoreType.DMA((4,))],
        compiler_params=pltpu.CompilerParams(vmem_limit_bytes=8 << 20),
        name="hold",
    )(in_hbm(weight))


def stack_rows(lhs, refs):
    at = 0
    for ref in refs:
        lhs[at : at + ref.shape[0], :] = ref[...]
        at += ref.shape[0]


def project_first_kernel(parts, *refs):
    att_refs, (w_ref, out_ref, lhs) = refs[:parts], refs[parts:]
    stack_rows(lhs, att_refs)
    out_ref[...] = nn(lhs[...], w_ref[...])


def project_first(pieces, weight):
    parts = len(pieces)
    tall = sum(piece.shape[0] for piece in pieces)
    width, cols = weight.shape
    vmem = pl.BlockSpec(memory_space=pltpu.VMEM)
    return pl.pallas_call(
        functools.partial(project_first_kernel, parts),
        out_shape=jax.ShapeDtypeStruct((tall, cols), jnp.float32),
        in_specs=[vmem] * (parts + 1),
        out_specs=vmem,
        scratch_shapes=[pltpu.VMEM((tall, width), jnp.bfloat16)],
        compiler_params=pltpu.CompilerParams(vmem_limit_bytes=8 << 20),
        cost_estimate=pl.CostEstimate(
            flops=2 * tall * width * cols,
            bytes_accessed=2 * width * cols,
            transcendentals=0,
        ),
        name="project_first",
    )(*pieces, weight)


def project_last_kernel(blocks, first_homes, homes, pos_ref, *refs):
    parts = len(homes)
    att_refs, (first_ref, w_ref, keep_ref, send_ref, lhs, both) = refs[:parts], refs[parts:]
    at = 0
    for home, start, size in first_homes:
        both[pos_ref[home], start : start + size, :] = first_ref[at : at + size, :]
        at += size
    stack_rows(lhs, att_refs)
    sums = nn(lhs[...], w_ref[...])
    at = 0
    for home, start, size in homes:
        both[pos_ref[home], start : start + size, :] = sums[at : at + size]
        at += size
    half = blocks // 2
    for k in range(half):
        keep_ref[k] = both[k]
        send_ref[k] = both[half + k]


def project_last(pieces, homes, first, first_homes, weight, pos, block):
    tall = sum(piece.shape[0] for piece in pieces)
    blocks = pos.shape[0]
    width, cols = weight.shape
    vmem = pl.BlockSpec(memory_space=pltpu.VMEM)
    shape = jax.ShapeDtypeStruct((blocks // 2, block, cols), jnp.float32)
    return pl.pallas_call(
        functools.partial(project_last_kernel, blocks, first_homes, homes),
        out_shape=(shape, shape),
        in_specs=[pl.BlockSpec(memory_space=pltpu.SMEM)] + [vmem] * (len(pieces) + 2),
        out_specs=(vmem, vmem),
        scratch_shapes=[
            pltpu.VMEM((tall, width), jnp.bfloat16),
            pltpu.VMEM((blocks, block, cols), jnp.float32),
        ],
        compiler_params=pltpu.CompilerParams(vmem_limit_bytes=8 << 20),
        cost_estimate=pl.CostEstimate(
            flops=2 * tall * width * cols,
            bytes_accessed=2 * width * cols,
            transcendentals=0,
        ),
        name="project_last",
    )(pos, *pieces, first, weight)


def exchange(x, size, flip):
    return lax.ppermute(x, "sample", [(i, i ^ flip) for i in range(size)])


def direct(
    queries, new_kv, gen_kv, prefix_kv, slot_prompt, prefix_blocks, gen_len, out_weight, size
):
    steps, rows, _ = queries.shape
    heads = new_kv.shape[2] // (2 * HD)
    me = lax.axis_index("sample")
    t = lax.axis_index("tensor")
    chip, core = t // 2, t % 2
    flips = (0, 1, 3, 2)
    payload = make_payload(prefix_kv, slot_prompt, prefix_blocks)
    far = exchange(payload, size, 3)
    near = exchange(payload, size, 1)
    grouped, acc, ml = gen_attention(queries, new_kv, gen_kv, gen_len, heads, 4)
    far, grouped, acc, ml = lax.optimization_barrier((far, grouped, acc, ml))
    diag = exchange(far, size, 1)
    most = add_slots(grouped, acc, ml, [payload, near, far], size, steps, heads)
    most_far = exchange(most, size, 3)
    most_near = exchange(most, size, 1)
    diag, _ = lax.optimization_barrier((diag, most))
    rest = add_slots(grouped, acc, ml, [diag], size, steps, heads)
    rest_far = exchange(rest, size, 3)
    rest_near = exchange(rest, size, 1)
    most_diag = exchange(most_far, size, 1)
    rest_diag = exchange(rest, size, 2)
    order = row_order([payload, near, far, diag], steps, rows)
    much, little = most.shape[0], rest.shape[0]
    held = hold(out_weight)
    first = project_first([most, rest, most_far, most_near], held)
    first_homes = ((0, 0, much), (0, much, little), (2, 0, much), (1, 0, much))
    last = [rest_far, rest_near, rest_diag, most_diag]
    homes = ((2, much, little), (1, much, little), (3, much, little), (3, 0, much))
    *last, first = lax.optimization_barrier((*last, first))
    pos = jnp.stack([me ^ flip for flip in flips]) ^ (2 * core + chip)
    keep, send = project_last(last, homes, first, first_homes, held, pos, much + little)
    got = lax.ppermute(send, "tensor", [(0, 1), (1, 0), (2, 3), (3, 2)])
    halves = (keep + got).astype(jnp.bfloat16)
    arrived = []
    for i in range(2):
        perm = []
        for c in range(size):
            for k in range(size):
                perm.append((c * size + k, (2 * (k % 2) + (i ^ (k // 2))) * size + c))
        piece = lax.ppermute(halves[i], ("sample", "tensor"), perm)
        arrived.append(piece)
    return finish(order, *arrived).reshape(steps, rows, -1)


def split_pairs(cache, heads):
    shaped = cache.reshape(cache.shape[:-1] + (heads, 2, HD))
    return (shaped[..., 0, :], shaped[..., 1, :])


def attend(queries, fresh, cached, prefix, valid, lengths, heads):
    steps_n, rows_n, width = queries.shape
    group = width // (heads * HD)
    scale = HD ** (-0.5)
    q_all = queries.reshape(steps_n, rows_n, heads, group, HD)
    pre_key, pre_val = split_pairs(prefix, heads)
    gen_key, gen_val = split_pairs(cached, heads)
    new_key, new_val = split_pairs(fresh, heads)
    s_pre = (
        jnp.einsum("srkgd,rpkd->srkgp", q_all, pre_key, preferred_element_type=jnp.float32) * scale
    )
    s_gen = (
        jnp.einsum("srkgd,rjkd->srkgj", q_all, gen_key, preferred_element_type=jnp.float32) * scale
    )
    s_new = (
        jnp.einsum("srkgd,urkd->srkgu", q_all, new_key, preferred_element_type=jnp.float32) * scale
    )
    m_pre = (jnp.arange(prefix.shape[1], dtype=jnp.int32)[None, :] < valid[:, None])[
        None, :, None, None, :
    ]
    m_gen = (jnp.arange(cached.shape[1], dtype=jnp.int32)[None, :] < lengths[:, None])[
        None, :, None, None, :
    ]
    order = jnp.arange(steps_n, dtype=jnp.int32)
    m_new = (order[None, :] <= order[:, None])[:, None, None, None, :]
    s_pre = jnp.where(m_pre, s_pre, -jnp.inf)
    s_gen = jnp.where(m_gen, s_gen, -jnp.inf)
    s_new = jnp.where(m_new, s_new, -jnp.inf)
    top = jnp.maximum(
        jnp.maximum(jnp.max(s_pre, -1, keepdims=True), jnp.max(s_gen, -1, keepdims=True)),
        jnp.max(s_new, -1, keepdims=True),
    )
    e_pre = jnp.exp(s_pre - top)
    e_gen = jnp.exp(s_gen - top)
    e_new = jnp.exp(s_new - top)
    total = (
        jnp.sum(e_pre, -1, keepdims=True)
        + jnp.sum(e_gen, -1, keepdims=True)
        + jnp.sum(e_new, -1, keepdims=True)
    )
    w_pre = (e_pre / total).astype(jnp.bfloat16)
    w_gen = (e_gen / total).astype(jnp.bfloat16)
    w_new = (e_new / total).astype(jnp.bfloat16)
    result = jnp.einsum("srkgp,rpkd->srkgd", w_pre, pre_val, preferred_element_type=jnp.float32)
    result = result + jnp.einsum(
        "srkgj,rjkd->srkgd", w_gen, gen_val, preferred_element_type=jnp.float32
    )
    result = result + jnp.einsum(
        "srkgu,urkd->srkgd", w_new, new_val, preferred_element_type=jnp.float32
    )
    return result.reshape(steps_n, rows_n, width).astype(jnp.bfloat16)


def shards(queries, new_kv, gen_kv, prefix_kv, slot_prompt, prefix_blocks, gen_len, out_weight):
    size = lax.axis_size("sample")
    fits = size == 4 and lax.axis_size("tensor") == 4 and prefix_kv.shape[0] == 1
    if fits and queries.shape[0] * queries.shape[1] % (16 * size) == 0:
        return direct(
            queries, new_kv, gen_kv, prefix_kv, slot_prompt, prefix_blocks, gen_len, out_weight, size
        )
    steps_n, rows_n, _ = queries.shape
    heads_local = new_kv.shape[2] // (2 * HD)
    all_prefix, all_slots, all_blocks = (
        lax.all_gather(prefix_kv, "sample", axis=0, tiled=True),
        lax.all_gather(slot_prompt, "sample", axis=0, tiled=True),
        lax.all_gather(prefix_blocks, "sample", axis=0, tiled=True),
    )
    prompt_total = all_slots.shape[0]
    inverse = (
        jnp.zeros((prompt_total,), jnp.int32)
        .at[all_slots]
        .set(jnp.arange(prompt_total, dtype=jnp.int32))
    )
    row_ids = lax.axis_index("sample") * rows_n + jnp.arange(rows_n, dtype=jnp.int32)
    picked = inverse[row_ids % prompt_total]
    own_prefix = jnp.take(all_prefix, picked, axis=0)
    valid = jnp.take(all_blocks, picked) * BLOCK
    attended = attend(queries, new_kv, gen_kv, own_prefix, valid, gen_len, heads_local)
    partial_sums = jnp.einsum(
        "srh,hc->src",
        attended,
        lax.all_gather(out_weight, "sample", axis=1, tiled=True),
        preferred_element_type=jnp.float32,
    )
    summed = []
    for step in range(steps_n):
        summed.append(
            lax.psum_scatter(partial_sums[step], "tensor", scatter_dimension=1, tiled=True)
        )
    mixed = jnp.stack(summed, axis=0)
    return mixed.astype(jnp.bfloat16)


def solution(mesh):
    in_specs = (
        P(None, ("groups", "sample"), "tensor"),
        P(None, ("groups", "sample"), "tensor"),
        P(("groups", "sample"), None, "tensor"),
        P(("groups", "sample"), None, "tensor"),
        P(("groups", "sample")),
        P(("groups", "sample")),
        P(("groups", "sample")),
        P("tensor", "sample"),
    )
    out_specs = P(None, ("groups", "sample"), "tensor")
    return jax.shard_map(
        shards, mesh=mesh, in_specs=in_specs, out_specs=out_specs, check_vma=False
    )
```

profile of v0, /device:TPU:1, one launch (start us, length us, event | category | flops | bytes accessed | tf_op | source)
XLA Modules:
  0.0 59.1 jit_solution(9354776478579085138)
XLA Ops:
  1.3 1.0 %make_payload.1.refs_0_ = bf16[1,264,512]{2,1,0:T(8,128)(2,1)S(1)} custom-call(s32[1]{0:T(128)S(6)} %copy.9.prompt_ref, s32[1]{0:T(128)S(6)} %copy.10.blocks_ref, bf16[1,256,512]{2,1,0:T(8,128)(2,1)} %pre_ref.1), custom_call_target="tpu_custom_call" | custom-call | tf_op jit(solution)/shard_map/make_payload/pallas_call | solution.py:42
  2.3 4.2 %collective-permute-start.1 = (bf16[1,264,512]{2,1,0:T(8,128)(2,1)S(1)}, bf16[1,264,512]{2,1,0:T(8,128)(2,1)S(1)}, u32[]{:S(2)}, u32[]{:S(2)}) collective-permute-start(bf16[1,264,512]{2,1,0:T(8,128)(2,1)S(1)} %make_payload.1.refs_0_), channel_id=1, source_target_pairs={{0,12},{4,8},{8,4},{12,0},{1,13},{5,9},{9,5},{13,1},{2,14},{6,10},... | collective-permute-start | bytes 811016 | tf_op jit(solution)/shard_map/ppermute | solution.py:372
  6.5 0.7 %copy-done = s32[16]{0:T(128)S(1)} copy-done((s32[16]{0:T(128)S(1)}, s32[16]{0:T(128)}, u32[]{:S(2)}) %copy-start) | copy-done | bytes 88
  7.1 7.5 %gen_attention.1 = (bf16[16,64,128]{2,1,0:T(8,128)(2,1)S(1)}, f32[16,64,128]{2,1,0:T(8,128)S(1)}, f32[16,64,128]{2,1,0:T(8,128)S(1)}) custom-call(s32[16]{0:T(128)S(1)} %copy-done, bf16[4,16,2048]{2,1,0:T(8,128)(2,1)} %q_ref.1, bf16[4,16,512]{2,1,0:T(8,128)(2,1)} %new_ref.1, bf16[16,512,512]{2,1,0:T(8,128)(2,1)} %kv_ref.1), custom_call_target="tpu_custom_call" | custom-call | flops 268435456 | bytes 8388608 | tf_op jit(solution)/shard_map/gen_attention/pallas_call | solution.py:130
  14.6 3.2 %collective-permute-start.2 = (bf16[1,264,512]{2,1,0:T(8,128)(2,1)S(1)}, bf16[1,264,512]{2,1,0:T(8,128)(2,1)S(1)}, u32[]{:S(2)}, u32[]{:S(2)}) collective-permute-start(bf16[1,264,512]{2,1,0:T(8,128)(2,1)S(1)} %collective-permute-done.1.refs_2_), channel_id=1, source_target_pairs={{0,4},{4,0},{8,12},{12,8},{1,5},{5,1},{9,13},{13,9},{2,6},{6,2},{1... | collective-permute-start | bytes 811016 | tf_op jit(solution)/shard_map/ppermute | solution.py:372
  17.8 1.5 %collective-permute-done.refs_1_ = bf16[1,264,512]{2,1,0:T(8,128)(2,1)S(1)} collective-permute-done((bf16[1,264,512]{2,1,0:T(8,128)(2,1)S(1)}, bf16[1,264,512]{2,1,0:T(8,128)(2,1)S(1)}, u32[]{:S(2)}, u32[]{:S(2)}) %collective-permute-start) | collective-permute-done | bytes 270368 | tf_op jit(solution)/shard_map/ppermute | solution.py:372
  19.3 2.6 %shard_map.82.refs_0_ = bf16[48,2048]{1,0:T(8,128)(2,1)S(1)} custom-call(bf16[1,264,512]{2,1,0:T(8,128)(2,1)S(1)} %make_payload.1.refs_0_, bf16[1,264,512]{2,1,0:T(8,128)(2,1)S(1)} %collective-permute-done.refs_1_, bf16[1,264,512]{2,1,0:T(8,128)(2,1)S(1)} %collective-permute-done.1.refs_2_, bf16[16,64,128]{2,1,0:T(8,128)(2,1)S(1)} %get-tuple-element.24.refs_3_.refs_1_, ...), custom_call_target="tpu_custom_call" | custom-call | flops 103809024 | bytes 811008 | tf_op jit(solution)/shard_map/pallas_call | solution.py:210
  21.9 0.6 collective-permute-start.6
  22.5 7.9 %collective-permute-done.6.refs_2_ = bf16[48,2048]{1,0:T(8,128)(2,1)S(1)} collective-permute-done((bf16[48,2048]{1,0:T(8,128)(2,1)S(1)}, bf16[48,2048]{1,0:T(8,128)(2,1)S(1)}, u32[]{:S(2)}, u32[]{:S(2)}) %collective-permute-start.6) | collective-permute-done | bytes 196640 | tf_op jit(solution)/shard_map/ppermute | solution.py:372
  30.4 0.6 %collective-permute-start.7 = (bf16[48,2048]{1,0:T(8,128)(2,1)S(1)}, bf16[48,2048]{1,0:T(8,128)(2,1)S(1)}, u32[]{:S(2)}, u32[]{:S(2)}) collective-permute-start(bf16[48,2048]{1,0:T(8,128)(2,1)S(1)} %collective-permute-done.6.refs_2_), channel_id=1, source_target_pairs={{0,4},{4,0},{8,12},{12,8},{1,5},{5,1},{9,13},{13,9},{2,6},{6,2},{1... | collective-permute-start | bytes 589832 | tf_op jit(solution)/shard_map/ppermute | solution.py:372
  31.0 0.9 %shard_map.83.refs_1_ = bf16[16,2048]{1,0:T(8,128)(2,1)S(1)} custom-call(bf16[1,264,512]{2,1,0:T(8,128)(2,1)S(1)} %collective-permute-done.2.refs_3_.refs_0_, bf16[16,64,128]{2,1,0:T(8,128)(2,1)S(1)} %get-tuple-element.24.refs_3_.refs_1_, f32[16,64,128]{2,1,0:T(8,128)S(1)} %get-tuple-element.25.refs_4_.refs_2_, ...), custom_call_target="tpu_custom_call" | custom-call | flops 34603008 | bytes 270336 | tf_op jit(solution)/shard_map/pallas_call | solution.py:210
  31.9 0.5 collective-permute-start.5
  32.9 2.6 %collective-permute-start.3 = (bf16[16,2048]{1,0:T(8,128)(2,1)S(1)}, bf16[16,2048]{1,0:T(8,128)(2,1)S(1)}, u32[]{:S(2)}, u32[]{:S(2)}) collective-permute-start(bf16[16,2048]{1,0:T(8,128)(2,1)S(1)} %shard_map.83.refs_1_), channel_id=1, source_target_pairs={{0,12},{4,8},{8,4},{12,0},{1,13},{5,9},{9,5},{13,1},{2,14},{6,10},... | collective-permute-start | bytes 196616 | tf_op jit(solution)/shard_map/ppermute | solution.py:372
  35.6 2.2 %hold.1.refs_4_.refs_5_ = bf16[2048,1024]{1,0:T(8,128)(2,1)S(1)} custom-call(bf16[2048,1024]{1,0:T(8,128)(2,1)} %w_ref.1), custom_call_target="tpu_custom_call" | custom-call | tf_op jit(solution)/shard_map/hold/pallas_call | solution.py:282
  37.9 0.9 %project_first.1.refs_4_ = f32[160,1024]{1,0:T(8,128)S(1)} custom-call(bf16[48,2048]{1,0:T(8,128)(2,1)S(1)} %shard_map.82.refs_0_, bf16[16,2048]{1,0:T(8,128)(2,1)S(1)} %shard_map.83.refs_1_, bf16[48,2048]{1,0:T(8,128)(2,1)S(1)} %collective-permute-done.6.refs_2_, bf16[48,2048]{1,0:T(8,128)(2,1)S(1)} %collective-permute-done.8.refs_3_, ...), custom_call_target="tpu_custom_call" | custom-call | flops 671088640 | bytes 4194304 | tf_op jit(solution)/shard_map/project_first/pallas_call | solution.py:311
  38.8 3.5 %collective-permute-done.3.refs_0_ = bf16[16,2048]{1,0:T(8,128)(2,1)S(1)} collective-permute-done((bf16[16,2048]{1,0:T(8,128)(2,1)S(1)}, bf16[16,2048]{1,0:T(8,128)(2,1)S(1)}, u32[]{:S(2)}, u32[]{:S(2)}) %collective-permute-start.3) | collective-permute-done | bytes 65568 | tf_op jit(solution)/shard_map/ppermute | solution.py:372
  42.3 1.4 %project_last.1 = (f32[2,64,1024]{2,1,0:T(8,128)S(1)}, f32[2,64,1024]{2,1,0:T(8,128)S(1)}) custom-call(s32[4]{0:T(128)S(1)} %add_xor_fusion.pos_ref, bf16[16,2048]{1,0:T(8,128)(2,1)S(1)} %collective-permute-done.3.refs_0_, bf16[16,2048]{1,0:T(8,128)(2,1)S(1)} %collective-permute-done.4.refs_1_, bf16[16,2048]{1,0:T(8,128)(2,1)S(1)} %collective-permute-done.5.refs_2_, ...), custom_call_target="tpu_custom_call" | custom-call | flops 402653184 | bytes 4194304 | tf_op jit(solution)/shard_map/project_last/pallas_call | solution.py:352
  43.7 2.0 %collective-permute-start.9 = (f32[2,64,1024]{2,1,0:T(8,128)S(1)}, f32[2,64,1024]{2,1,0:T(8,128)S(1)}, u32[]{:S(2)}, u32[]{:S(2)}) collective-permute-start(f32[2,64,1024]{2,1,0:T(8,128)S(1)} %get-tuple-element.34), channel_id=1, source_target_pairs={{0,1},{1,0},{2,3},{3,2},{4,5},{5,4},{6,7},{7,6},{8,9},{9,8},{10,11... | collective-permute-start | bytes 1572872 | tf_op jit(solution)/shard_map/ppermute | solution.py:409
  45.7 1.5 %collective-permute-done.9 = f32[2,64,1024]{2,1,0:T(8,128)S(1)} collective-permute-done((f32[2,64,1024]{2,1,0:T(8,128)S(1)}, f32[2,64,1024]{2,1,0:T(8,128)S(1)}, u32[]{:S(2)}, u32[]{:S(2)}) %collective-permute-start.9) | collective-permute-done | bytes 524320 | tf_op jit(solution)/shard_map/ppermute | solution.py:409
  47.3 1.8 %collective-permute-start.11 = (bf16[64,1024]{1,0:T(8,128)(2,1)S(1)}, bf16[64,1024]{1,0:T(8,128)(2,1)S(1)}, u32[]{:S(2)}, u32[]{:S(2)}) collective-permute-start(bf16[64,1024]{1,0:T(8,128)(2,1)S(1)} %get-tuple-element.35), channel_id=1, source_target_pairs={{0,4},{1,12},{2,0},{3,8},{4,5},{5,13},{6,1},{7,9},{8,6},{9,14},{10... | collective-permute-start | bytes 393224 | tf_op jit(solution)/shard_map/ppermute | solution.py:417
  49.2 2.2 %collective-permute-start.10 = (bf16[64,1024]{1,0:T(8,128)(2,1)S(1)}, bf16[64,1024]{1,0:T(8,128)(2,1)S(1)}, u32[]{:S(2)}, u32[]{:S(2)}) collective-permute-start(bf16[64,1024]{1,0:T(8,128)(2,1)S(1)} %get-tuple-element.36), channel_id=1, source_target_pairs={{0,0},{1,8},{2,4},{3,12},{4,1},{5,9},{6,5},{7,13},{8,2},{9,10},{10... | collective-permute-start | bytes 393224 | tf_op jit(solution)/shard_map/ppermute | solution.py:417
  51.5 3.7 %collective-permute-done.11.b_ref = bf16[64,1024]{1,0:T(8,128)(2,1)S(1)} collective-permute-done((bf16[64,1024]{1,0:T(8,128)(2,1)S(1)}, bf16[64,1024]{1,0:T(8,128)(2,1)S(1)}, u32[]{:S(2)}, u32[]{:S(2)}) %collective-permute-start.11) | collective-permute-done | bytes 131104 | tf_op jit(solution)/shard_map/ppermute | solution.py:417
  55.2 3.0 %collective-permute-done.10.a_ref = bf16[64,1024]{1,0:T(8,128)(2,1)S(1)} collective-permute-done((bf16[64,1024]{1,0:T(8,128)(2,1)S(1)}, bf16[64,1024]{1,0:T(8,128)(2,1)S(1)}, u32[]{:S(2)}, u32[]{:S(2)}) %collective-permute-start.10) | collective-permute-done | bytes 131104 | tf_op jit(solution)/shard_map/ppermute | solution.py:417
  58.2 0.8 %finish.1 = bf16[64,1024]{1,0:T(8,128)(2,1)} custom-call(bf16[64,64]{1,0:T(8,128)(2,1)S(1)} %row_order.1.order_ref, bf16[64,1024]{1,0:T(8,128)(2,1)S(1)} %collective-permute-done.10.a_ref, bf16[64,1024]{1,0:T(8,128)(2,1)S(1)} %collective-permute-done.11.b_ref), custom_call_target="tpu_custom_call" | custom-call | tf_op jit(solution)/shard_map/finish/pallas_call | solution.py:260
  (14 shorter events, 0.8 us)
Async XLA Ops:
  2.3 12.4 %collective-permute-start.1 = (bf16[1,264,512]{2,1,0:T(8,128)(2,1)S(1)}, bf16[1,264,512]{2,1,0:T(8,128)(2,1)S(1)}, u32[]{:S(2)}, u32[]{:S(2)}) collective-permute-start(bf16[1,264,512]{2,1,0:T(8,128)(2,1)S(1)} %make_payload.1.refs_0_), channel_id=1, source_target_pairs={{0,12},{4,8},{8,4},{12,0},{1,13},{5,9},{9,5},{13,1},{2,14},{6,10},... | collective-permute-start | bytes 811016 | tf_op jit(solution)/shard_map/ppermute | solution.py:372
  6.5 12.8 %collective-permute-start = (bf16[1,264,512]{2,1,0:T(8,128)(2,1)S(1)}, bf16[1,264,512]{2,1,0:T(8,128)(2,1)S(1)}, u32[]{:S(2)}, u32[]{:S(2)}) collective-permute-start(bf16[1,264,512]{2,1,0:T(8,128)(2,1)S(1)} %make_payload.1.refs_0_), channel_id=1, source_target_pairs={{0,4},{4,0},{8,12},{12,8},{1,5},{5,1},{9,13},{13,9},{2,6},{6,2},{1... | collective-permute-start | bytes 811016 | tf_op jit(solution)/shard_map/ppermute | solution.py:372
  6.5 0.7 %copy-start = (s32[16]{0:T(128)S(1)}, s32[16]{0:T(128)}, u32[]{:S(2)}) copy-start(s32[16]{0:T(128)} %len_ref.1) | copy-start | bytes 196
  14.6 16.4 %collective-permute-start.2 = (bf16[1,264,512]{2,1,0:T(8,128)(2,1)S(1)}, bf16[1,264,512]{2,1,0:T(8,128)(2,1)S(1)}, u32[]{:S(2)}, u32[]{:S(2)}) collective-permute-start(bf16[1,264,512]{2,1,0:T(8,128)(2,1)S(1)} %collective-permute-done.1.refs_2_), channel_id=1, source_target_pairs={{0,4},{4,0},{8,12},{12,8},{1,5},{5,1},{9,13},{13,9},{2,6},{6,2},{1... | collective-permute-start | bytes 811016 | tf_op jit(solution)/shard_map/ppermute | solution.py:372
  21.9 8.5 %collective-permute-start.6 = (bf16[48,2048]{1,0:T(8,128)(2,1)S(1)}, bf16[48,2048]{1,0:T(8,128)(2,1)S(1)}, u32[]{:S(2)}, u32[]{:S(2)}) collective-permute-start(bf16[48,2048]{1,0:T(8,128)(2,1)S(1)} %shard_map.82.refs_0_), channel_id=1, source_target_pairs={{0,12},{4,8},{8,4},{12,0},{1,13},{5,9},{9,5},{13,1},{2,14},{6,10},... | collective-permute-start | bytes 589832 | tf_op jit(solution)/shard_map/ppermute | solution.py:372
  22.5 15.4 %collective-permute-start.8 = (bf16[48,2048]{1,0:T(8,128)(2,1)S(1)}, bf16[48,2048]{1,0:T(8,128)(2,1)S(1)}, u32[]{:S(2)}, u32[]{:S(2)}) collective-permute-start(bf16[48,2048]{1,0:T(8,128)(2,1)S(1)} %shard_map.82.refs_0_), channel_id=1, source_target_pairs={{0,4},{4,0},{8,12},{12,8},{1,5},{5,1},{9,13},{13,9},{2,6},{6,2},{1... | collective-permute-start | bytes 589832 | tf_op jit(solution)/shard_map/ppermute | solution.py:372
  30.4 11.9 %collective-permute-start.7 = (bf16[48,2048]{1,0:T(8,128)(2,1)S(1)}, bf16[48,2048]{1,0:T(8,128)(2,1)S(1)}, u32[]{:S(2)}, u32[]{:S(2)}) collective-permute-start(bf16[48,2048]{1,0:T(8,128)(2,1)S(1)} %collective-permute-done.6.refs_2_), channel_id=1, source_target_pairs={{0,4},{4,0},{8,12},{12,8},{1,5},{5,1},{9,13},{13,9},{2,6},{6,2},{1... | collective-permute-start | bytes 589832 | tf_op jit(solution)/shard_map/ppermute | solution.py:372
  31.9 6.8 %collective-permute-start.5 = (bf16[16,2048]{1,0:T(8,128)(2,1)S(1)}, bf16[16,2048]{1,0:T(8,128)(2,1)S(1)}, u32[]{:S(2)}, u32[]{:S(2)}) collective-permute-start(bf16[16,2048]{1,0:T(8,128)(2,1)S(1)} %shard_map.83.refs_1_), channel_id=1, source_target_pairs={{0,8},{4,12},{8,0},{12,4},{1,9},{5,13},{9,1},{13,5},{2,10},{6,14},... | collective-permute-start | bytes 196616 | tf_op jit(solution)/shard_map/ppermute | solution.py:372
  32.5 6.3 %collective-permute-start.4 = (bf16[16,2048]{1,0:T(8,128)(2,1)S(1)}, bf16[16,2048]{1,0:T(8,128)(2,1)S(1)}, u32[]{:S(2)}, u32[]{:S(2)}) collective-permute-start(bf16[16,2048]{1,0:T(8,128)(2,1)S(1)} %shard_map.83.refs_1_), channel_id=1, source_target_pairs={{0,4},{4,0},{8,12},{12,8},{1,5},{5,1},{9,13},{13,9},{2,6},{6,2},{1... | collective-permute-start | bytes 196616 | tf_op jit(solution)/shard_map/ppermute | solution.py:372
  32.9 9.3 %collective-permute-start.3 = (bf16[16,2048]{1,0:T(8,128)(2,1)S(1)}, bf16[16,2048]{1,0:T(8,128)(2,1)S(1)}, u32[]{:S(2)}, u32[]{:S(2)}) collective-permute-start(bf16[16,2048]{1,0:T(8,128)(2,1)S(1)} %shard_map.83.refs_1_), channel_id=1, source_target_pairs={{0,12},{4,8},{8,4},{12,0},{1,13},{5,9},{9,5},{13,1},{2,14},{6,10},... | collective-permute-start | bytes 196616 | tf_op jit(solution)/shard_map/ppermute | solution.py:372
  43.7 3.5 %collective-permute-start.9 = (f32[2,64,1024]{2,1,0:T(8,128)S(1)}, f32[2,64,1024]{2,1,0:T(8,128)S(1)}, u32[]{:S(2)}, u32[]{:S(2)}) collective-permute-start(f32[2,64,1024]{2,1,0:T(8,128)S(1)} %get-tuple-element.34), channel_id=1, source_target_pairs={{0,1},{1,0},{2,3},{3,2},{4,5},{5,4},{6,7},{7,6},{8,9},{9,8},{10,11... | collective-permute-start | bytes 1572872 | tf_op jit(solution)/shard_map/ppermute | solution.py:409
  47.3 7.9 %collective-permute-start.11 = (bf16[64,1024]{1,0:T(8,128)(2,1)S(1)}, bf16[64,1024]{1,0:T(8,128)(2,1)S(1)}, u32[]{:S(2)}, u32[]{:S(2)}) collective-permute-start(bf16[64,1024]{1,0:T(8,128)(2,1)S(1)} %get-tuple-element.35), channel_id=1, source_target_pairs={{0,4},{1,12},{2,0},{3,8},{4,5},{5,13},{6,1},{7,9},{8,6},{9,14},{10... | collective-permute-start | bytes 393224 | tf_op jit(solution)/shard_map/ppermute | solution.py:417
  49.2 9.1 %collective-permute-start.10 = (bf16[64,1024]{1,0:T(8,128)(2,1)S(1)}, bf16[64,1024]{1,0:T(8,128)(2,1)S(1)}, u32[]{:S(2)}, u32[]{:S(2)}) collective-permute-start(bf16[64,1024]{1,0:T(8,128)(2,1)S(1)} %get-tuple-element.36), channel_id=1, source_target_pairs={{0,0},{1,8},{2,4},{3,12},{4,1},{5,9},{6,5},{7,13},{8,2},{9,10},{10... | collective-permute-start | bytes 393224 | tf_op jit(solution)/shard_map/ppermute | solution.py:417
where the time goes:
time: 59.3 us; the launch traced here: 59.1 us
  waiting for transfers between devices  21.3 us (36%)
  starting transfers between devices  18.2 us (31%)
  Pallas kernels  17.4 us (29%)
  between operations  1.41 us (2%)
  local copies, waits for them, and re-layouts  0.67 us (1%)
    ppermute x9, waiting for transfers between devices, exchange(): return lax.ppermute(x, 'sample', [(i, i ^ flip) for i in range(size)])  13 us
    ppermute x9, starting transfers between devices, exchange(): return lax.ppermute(x, 'sample', [(i, i ^ flip) for i in range(size)])  12.2 us
    pallas_call x1, Pallas kernels, gen_attention(): pl.pallas_call(functools.partial(gen_kernel, steps, heads, group), out_sh...  7.49 us
    ppermute x2, waiting for transfers between devices, direct(): piece = lax.ppermute(halves[i], ('sample', 'tensor'), perm)  6.73 us
    ppermute x2, starting transfers between devices, direct(): piece = lax.ppermute(halves[i], ('sample', 'tensor'), perm)  4.05 us
    pallas_call x2, Pallas kernels, add_slots(): pl.pallas_call(functools.partial(add_slots_kernel, slots, steps, group, c...  3.49 us
    pallas_call x1, Pallas kernels, hold(): pl.pallas_call(hold_kernel, out_shape=jax.ShapeDtypeStruct(weight.shape,...  2.21 us
    ppermute x1, starting transfers between devices, direct(): got = lax.ppermute(send, 'tensor', [(0, 1), (1, 0), (2, 3), (3, 2)])  1.96 us
  transfers between devices with their start and end apart: 12, of which 6 were waited for; matrix products, arithmetic and copies ran while one was open for 0% of the time, Pallas kernels for 24%

commit v1 on v0

--- a/solution.py
+++ b/solution.py
@@ -12,6 +12,7 @@
 BLOCK = 128
 LOW = -1e30
 EXTRA = 8
+MIX = 3
 
 
 def nt(a, b):
@@ -404,7 +405,7 @@
     last = [rest_far, rest_near, rest_diag, most_diag]
     homes = ((2, much, little), (1, much, little), (3, much, little), (3, 0, much))
     *last, first = lax.optimization_barrier((*last, first))
-    pos = jnp.stack([me ^ flip for flip in flips]) ^ (2 * core + chip)
+    pos = jnp.stack([me ^ flip for flip in flips]) ^ (2 * core + chip) ^ MIX
     keep, send = project_last(last, homes, first, first_homes, held, pos, much + little)
     got = lax.ppermute(send, "tensor", [(0, 1), (1, 0), (2, 3), (3, 2)])
     halves = (keep + got).astype(jnp.bfloat16)
@@ -413,7 +414,7 @@
         perm = []
         for c in range(size):
             for k in range(size):
-                perm.append((c * size + k, (2 * (k % 2) + (i ^ (k // 2))) * size + c))
+                perm.append((c * size + k, (2 * (k % 2) + (i ^ (k // 2)) ^ MIX) * size + c))
         piece = lax.ppermute(halves[i], ("sample", "tensor"), perm)
         arrived.append(piece)
     return finish(order, *arrived).reshape(steps, rows, -1)

time: 59.3 us -> 57.1 us (0.963)
  the two profiles are of different devices: /device:TPU:1 before, /device:TPU:0 now
where the time goes in v1:
time: 57.1 us; the launch traced here: 56.3 us
  starting transfers between devices  21.5 us (38%)
  Pallas kernels  17.4 us (30%)
  waiting for transfers between devices  15.1 us (26%)
  between operations  1.43 us (3%)
  local copies, waits for them, and re-layouts  0.67 us (1%)
    ppermute x9, starting transfers between devices, exchange(): return lax.ppermute(x, 'sample', [(i, i ^ flip) for i in range(size)])  17.5 us
    ppermute x9, waiting for transfers between devices, exchange(): return lax.ppermute(x, 'sample', [(i, i ^ flip) for i in range(size)])  9.54 us
    pallas_call x1, Pallas kernels, gen_attention(): pl.pallas_call(functools.partial(gen_kernel, steps, heads, group), out_sh...  7.49 us
    ppermute x2, starting transfers between devices, direct(): piece = lax.ppermute(halves[i], ('sample', 'tensor'), perm)  3.94 us
    ppermute x2, waiting for transfers between devices, direct(): piece = lax.ppermute(halves[i], ('sample', 'tensor'), perm)  3.66 us
    pallas_call x2, Pallas kernels, add_slots(): pl.pallas_call(functools.partial(add_slots_kernel, slots, steps, group, c...  3.49 us
    pallas_call x1, Pallas kernels, hold(): pl.pallas_call(hold_kernel, out_shape=jax.ShapeDtypeStruct(weight.shape,...  2.21 us
    ppermute x1, waiting for transfers between devices, direct(): got = lax.ppermute(send, 'tensor', [(0, 1), (1, 0), (2, 3), (3, 2)])  1.9 us
  transfers between devices with their start and end apart: 12, of which 5 were waited for; matrix products, arithmetic and copies ran while one was open for 0% of the time, Pallas kernels for 25%

profile of v1, /device:TPU:0, one launch (start us, length us, event | category | flops | bytes accessed | tf_op | source)
XLA Modules:
  0.0 56.3 jit_solution(17537504848677834676)
XLA Ops:
  1.3 1.0 %make_payload.1.refs_0_ = bf16[1,264,512]{2,1,0:T(8,128)(2,1)S(1)} custom-call(s32[1]{0:T(128)S(6)} %copy.9.prompt_ref, s32[1]{0:T(128)S(6)} %copy.10.blocks_ref, bf16[1,256,512]{2,1,0:T(8,128)(2,1)} %pre_ref.1), custom_call_target="tpu_custom_call" | custom-call | tf_op jit(solution)/shard_map/make_payload/pallas_call | solution.py:43
  2.3 5.1 %collective-permute-start.1 = (bf16[1,264,512]{2,1,0:T(8,128)(2,1)S(1)}, bf16[1,264,512]{2,1,0:T(8,128)(2,1)S(1)}, u32[]{:S(2)}, u32[]{:S(2)}) collective-permute-start(bf16[1,264,512]{2,1,0:T(8,128)(2,1)S(1)} %make_payload.1.refs_0_), channel_id=1, source_target_pairs={{0,12},{4,8},{8,4},{12,0},{1,13},{5,9},{9,5},{13,1},{2,14},{6,10},... | collective-permute-start | bytes 811016 | tf_op jit(solution)/shard_map/ppermute | solution.py:373
  7.4 0.7 %copy-done = s32[16]{0:T(128)S(1)} copy-done((s32[16]{0:T(128)S(1)}, s32[16]{0:T(128)}, u32[]{:S(2)}) %copy-start) | copy-done | bytes 88
  8.1 7.5 %gen_attention.1 = (bf16[16,64,128]{2,1,0:T(8,128)(2,1)S(1)}, f32[16,64,128]{2,1,0:T(8,128)S(1)}, f32[16,64,128]{2,1,0:T(8,128)S(1)}) custom-call(s32[16]{0:T(128)S(1)} %copy-done, bf16[4,16,2048]{2,1,0:T(8,128)(2,1)} %q_ref.1, bf16[4,16,512]{2,1,0:T(8,128)(2,1)} %new_ref.1, bf16[16,512,512]{2,1,0:T(8,128)(2,1)} %kv_ref.1), custom_call_target="tpu_custom_call" | custom-call | flops 268435456 | bytes 8388608 | tf_op jit(solution)/shard_map/gen_attention/pallas_call | solution.py:131
  15.6 3.8 %collective-permute-start.2 = (bf16[1,264,512]{2,1,0:T(8,128)(2,1)S(1)}, bf16[1,264,512]{2,1,0:T(8,128)(2,1)S(1)}, u32[]{:S(2)}, u32[]{:S(2)}) collective-permute-start(bf16[1,264,512]{2,1,0:T(8,128)(2,1)S(1)} %collective-permute-done.1.refs_2_), channel_id=1, source_target_pairs={{0,4},{4,0},{8,12},{12,8},{1,5},{5,1},{9,13},{13,9},{2,6},{6,2},{1... | collective-permute-start | bytes 811016 | tf_op jit(solution)/shard_map/ppermute | solution.py:373
  19.4 0.5 collective-permute-done.refs_1_
  19.9 2.6 %shard_map.82.refs_0_ = bf16[48,2048]{1,0:T(8,128)(2,1)S(1)} custom-call(bf16[1,264,512]{2,1,0:T(8,128)(2,1)S(1)} %make_payload.1.refs_0_, bf16[1,264,512]{2,1,0:T(8,128)(2,1)S(1)} %collective-permute-done.refs_1_, bf16[1,264,512]{2,1,0:T(8,128)(2,1)S(1)} %collective-permute-done.1.refs_2_, bf16[16,64,128]{2,1,0:T(8,128)(2,1)S(1)} %get-tuple-element.24.refs_3_.refs_1_, ...), custom_call_target="tpu_custom_call" | custom-call | flops 103809024 | bytes 811008 | tf_op jit(solution)/shard_map/pallas_call | solution.py:211
  22.5 2.1 %collective-permute-start.6 = (bf16[48,2048]{1,0:T(8,128)(2,1)S(1)}, bf16[48,2048]{1,0:T(8,128)(2,1)S(1)}, u32[]{:S(2)}, u32[]{:S(2)}) collective-permute-start(bf16[48,2048]{1,0:T(8,128)(2,1)S(1)} %shard_map.82.refs_0_), channel_id=1, source_target_pairs={{0,12},{4,8},{8,4},{12,0},{1,13},{5,9},{9,5},{13,1},{2,14},{6,10},... | collective-permute-start | bytes 589832 | tf_op jit(solution)/shard_map/ppermute | solution.py:373
  24.5 7.6 %collective-permute-done.6.refs_2_ = bf16[48,2048]{1,0:T(8,128)(2,1)S(1)} collective-permute-done((bf16[48,2048]{1,0:T(8,128)(2,1)S(1)}, bf16[48,2048]{1,0:T(8,128)(2,1)S(1)}, u32[]{:S(2)}, u32[]{:S(2)}) %collective-permute-start.6) | collective-permute-done | bytes 196640 | tf_op jit(solution)/shard_map/ppermute | solution.py:373
  32.2 2.0 %collective-permute-start.7 = (bf16[48,2048]{1,0:T(8,128)(2,1)S(1)}, bf16[48,2048]{1,0:T(8,128)(2,1)S(1)}, u32[]{:S(2)}, u32[]{:S(2)}) collective-permute-start(bf16[48,2048]{1,0:T(8,128)(2,1)S(1)} %collective-permute-done.6.refs_2_), channel_id=1, source_target_pairs={{0,4},{4,0},{8,12},{12,8},{1,5},{5,1},{9,13},{13,9},{2,6},{6,2},{1... | collective-permute-start | bytes 589832 | tf_op jit(solution)/shard_map/ppermute | solution.py:373
  34.2 0.9 %shard_map.83.refs_1_ = bf16[16,2048]{1,0:T(8,128)(2,1)S(1)} custom-call(bf16[1,264,512]{2,1,0:T(8,128)(2,1)S(1)} %collective-permute-done.2.refs_3_.refs_0_, bf16[16,64,128]{2,1,0:T(8,128)(2,1)S(1)} %get-tuple-element.24.refs_3_.refs_1_, f32[16,64,128]{2,1,0:T(8,128)S(1)} %get-tuple-element.25.refs_4_.refs_2_, ...), custom_call_target="tpu_custom_call" | custom-call | flops 34603008 | bytes 270336 | tf_op jit(solution)/shard_map/pallas_call | solution.py:211
  35.1 1.2 %collective-permute-start.5 = (bf16[16,2048]{1,0:T(8,128)(2,1)S(1)}, bf16[16,2048]{1,0:T(8,128)(2,1)S(1)}, u32[]{:S(2)}, u32[]{:S(2)}) collective-permute-start(bf16[16,2048]{1,0:T(8,128)(2,1)S(1)} %shard_map.83.refs_1_), channel_id=1, source_target_pairs={{0,8},{4,12},{8,0},{12,4},{1,9},{5,13},{9,1},{13,5},{2,10},{6,14},... | collective-permute-start | bytes 196616 | tf_op jit(solution)/shard_map/ppermute | solution.py:373
  36.3 0.6 %collective-permute-start.4 = (bf16[16,2048]{1,0:T(8,128)(2,1)S(1)}, bf16[16,2048]{1,0:T(8,128)(2,1)S(1)}, u32[]{:S(2)}, u32[]{:S(2)}) collective-permute-start(bf16[16,2048]{1,0:T(8,128)(2,1)S(1)} %shard_map.83.refs_1_), channel_id=1, source_target_pairs={{0,4},{4,0},{8,12},{12,8},{1,5},{5,1},{9,13},{13,9},{2,6},{6,2},{1... | collective-permute-start | bytes 196616 | tf_op jit(solution)/shard_map/ppermute | solution.py:373
  36.9 2.6 %collective-permute-start.3 = (bf16[16,2048]{1,0:T(8,128)(2,1)S(1)}, bf16[16,2048]{1,0:T(8,128)(2,1)S(1)}, u32[]{:S(2)}, u32[]{:S(2)}) collective-permute-start(bf16[16,2048]{1,0:T(8,128)(2,1)S(1)} %shard_map.83.refs_1_), channel_id=1, source_target_pairs={{0,12},{4,8},{8,4},{12,0},{1,13},{5,9},{9,5},{13,1},{2,14},{6,10},... | collective-permute-start | bytes 196616 | tf_op jit(solution)/shard_map/ppermute | solution.py:373
  39.5 0.1 fusion.pos_ref
  39.6 2.2 %hold.1.refs_4_.refs_5_ = bf16[2048,1024]{1,0:T(8,128)(2,1)S(1)} custom-call(bf16[2048,1024]{1,0:T(8,128)(2,1)} %w_ref.1), custom_call_target="tpu_custom_call" | custom-call | tf_op jit(solution)/shard_map/hold/pallas_call | solution.py:283
  41.8 0.9 %project_first.1.refs_4_ = f32[160,1024]{1,0:T(8,128)S(1)} custom-call(bf16[48,2048]{1,0:T(8,128)(2,1)S(1)} %shard_map.82.refs_0_, bf16[16,2048]{1,0:T(8,128)(2,1)S(1)} %shard_map.83.refs_1_, bf16[48,2048]{1,0:T(8,128)(2,1)S(1)} %collective-permute-done.6.refs_2_, bf16[48,2048]{1,0:T(8,128)(2,1)S(1)} %collective-permute-done.8.refs_3_, ...), custom_call_target="tpu_custom_call" | custom-call | flops 671088640 | bytes 4194304 | tf_op jit(solution)/shard_map/project_first/pallas_call | solution.py:312
  42.7 1.4 %collective-permute-done.3.refs_0_ = bf16[16,2048]{1,0:T(8,128)(2,1)S(1)} collective-permute-done((bf16[16,2048]{1,0:T(8,128)(2,1)S(1)}, bf16[16,2048]{1,0:T(8,128)(2,1)S(1)}, u32[]{:S(2)}, u32[]{:S(2)}) %collective-permute-start.3) | collective-permute-done | bytes 65568 | tf_op jit(solution)/shard_map/ppermute | solution.py:373
  44.2 1.4 %project_last.1 = (f32[2,64,1024]{2,1,0:T(8,128)S(1)}, f32[2,64,1024]{2,1,0:T(8,128)S(1)}) custom-call(s32[4]{0:T(128)S(1)} %fusion.pos_ref, bf16[16,2048]{1,0:T(8,128)(2,1)S(1)} %collective-permute-done.3.refs_0_, bf16[16,2048]{1,0:T(8,128)(2,1)S(1)} %collective-permute-done.4.refs_1_, bf16[16,2048]{1,0:T(8,128)(2,1)S(1)} %collective-permute-done.5.refs_2_, ...), custom_call_target="tpu_custom_call" | custom-call | flops 402653184 | bytes 4194304 | tf_op jit(solution)/shard_map/project_last/pallas_call | solution.py:353
  45.7 1.9 %collective-permute-done.9 = f32[2,64,1024]{2,1,0:T(8,128)S(1)} collective-permute-done((f32[2,64,1024]{2,1,0:T(8,128)S(1)}, f32[2,64,1024]{2,1,0:T(8,128)S(1)}, u32[]{:S(2)}, u32[]{:S(2)}) %collective-permute-start.9) | collective-permute-done | bytes 524320 | tf_op jit(solution)/shard_map/ppermute | solution.py:410
  47.8 3.9 %collective-permute-start.10 = (bf16[64,1024]{1,0:T(8,128)(2,1)S(1)}, bf16[64,1024]{1,0:T(8,128)(2,1)S(1)}, u32[]{:S(2)}, u32[]{:S(2)}) collective-permute-start(bf16[64,1024]{1,0:T(8,128)(2,1)S(1)} %get-tuple-element.36), channel_id=1, source_target_pairs={{0,12},{1,4},{2,8},{3,0},{4,13},{5,5},{6,9},{7,1},{8,14},{9,6},{10... | collective-permute-start | bytes 393224 | tf_op jit(solution)/shard_map/ppermute | solution.py:418
  51.6 0.1 row_order.1.order_ref
  51.8 3.7 %collective-permute-done.10.a_ref = bf16[64,1024]{1,0:T(8,128)(2,1)S(1)} collective-permute-done((bf16[64,1024]{1,0:T(8,128)(2,1)S(1)}, bf16[64,1024]{1,0:T(8,128)(2,1)S(1)}, u32[]{:S(2)}, u32[]{:S(2)}) %collective-permute-start.10) | collective-permute-done | bytes 131104 | tf_op jit(solution)/shard_map/ppermute | solution.py:418
  55.4 0.8 %finish.1 = bf16[64,1024]{1,0:T(8,128)(2,1)} custom-call(bf16[64,64]{1,0:T(8,128)(2,1)S(1)} %row_order.1.order_ref, bf16[64,1024]{1,0:T(8,128)(2,1)S(1)} %collective-permute-done.10.a_ref, bf16[64,1024]{1,0:T(8,128)(2,1)S(1)} %collective-permute-done.11.b_ref), custom_call_target="tpu_custom_call" | custom-call | tf_op jit(solution)/shard_map/finish/pallas_call | solution.py:261
  (14 shorter events, 0.2 us)
Async XLA Ops:
  2.3 13.3 %collective-permute-start.1 = (bf16[1,264,512]{2,1,0:T(8,128)(2,1)S(1)}, bf16[1,264,512]{2,1,0:T(8,128)(2,1)S(1)}, u32[]{:S(2)}, u32[]{:S(2)}) collective-permute-start(bf16[1,264,512]{2,1,0:T(8,128)(2,1)S(1)} %make_payload.1.refs_0_), channel_id=1, source_target_pairs={{0,12},{4,8},{8,4},{12,0},{1,13},{5,9},{9,5},{13,1},{2,14},{6,10},... | collective-permute-start | bytes 811016 | tf_op jit(solution)/shard_map/ppermute | solution.py:373
  7.4 12.5 %collective-permute-start = (bf16[1,264,512]{2,1,0:T(8,128)(2,1)S(1)}, bf16[1,264,512]{2,1,0:T(8,128)(2,1)S(1)}, u32[]{:S(2)}, u32[]{:S(2)}) collective-permute-start(bf16[1,264,512]{2,1,0:T(8,128)(2,1)S(1)} %make_payload.1.refs_0_), channel_id=1, source_target_pairs={{0,4},{4,0},{8,12},{12,8},{1,5},{5,1},{9,13},{13,9},{2,6},{6,2},{1... | collective-permute-start | bytes 811016 | tf_op jit(solution)/shard_map/ppermute | solution.py:373
  7.4 0.7 %copy-start = (s32[16]{0:T(128)S(1)}, s32[16]{0:T(128)}, u32[]{:S(2)}) copy-start(s32[16]{0:T(128)} %len_ref.1) | copy-start | bytes 196
  15.6 18.6 %collective-permute-start.2 = (bf16[1,264,512]{2,1,0:T(8,128)(2,1)S(1)}, bf16[1,264,512]{2,1,0:T(8,128)(2,1)S(1)}, u32[]{:S(2)}, u32[]{:S(2)}) collective-permute-start(bf16[1,264,512]{2,1,0:T(8,128)(2,1)S(1)} %collective-permute-done.1.refs_2_), channel_id=1, source_target_pairs={{0,4},{4,0},{8,12},{12,8},{1,5},{5,1},{9,13},{13,9},{2,6},{6,2},{1... | collective-permute-start | bytes 811016 | tf_op jit(solution)/shard_map/ppermute | solution.py:373
  22.5 9.7 %collective-permute-start.6 = (bf16[48,2048]{1,0:T(8,128)(2,1)S(1)}, bf16[48,2048]{1,0:T(8,128)(2,1)S(1)}, u32[]{:S(2)}, u32[]{:S(2)}) collective-permute-start(bf16[48,2048]{1,0:T(8,128)(2,1)S(1)} %shard_map.82.refs_0_), channel_id=1, source_target_pairs={{0,12},{4,8},{8,4},{12,0},{1,13},{5,9},{9,5},{13,1},{2,14},{6,10},... | collective-permute-start | bytes 589832 | tf_op jit(solution)/shard_map/ppermute | solution.py:373
  24.5 17.3 %collective-permute-start.8 = (bf16[48,2048]{1,0:T(8,128)(2,1)S(1)}, bf16[48,2048]{1,0:T(8,128)(2,1)S(1)}, u32[]{:S(2)}, u32[]{:S(2)}) collective-permute-start(bf16[48,2048]{1,0:T(8,128)(2,1)S(1)} %shard_map.82.refs_0_), channel_id=1, source_target_pairs={{0,4},{4,0},{8,12},{12,8},{1,5},{5,1},{9,13},{13,9},{2,6},{6,2},{1... | collective-permute-start | bytes 589832 | tf_op jit(solution)/shard_map/ppermute | solution.py:373
  32.2 12.0 %collective-permute-start.7 = (bf16[48,2048]{1,0:T(8,128)(2,1)S(1)}, bf16[48,2048]{1,0:T(8,128)(2,1)S(1)}, u32[]{:S(2)}, u32[]{:S(2)}) collective-permute-start(bf16[48,2048]{1,0:T(8,128)(2,1)S(1)} %collective-permute-done.6.refs_2_), channel_id=1, source_target_pairs={{0,4},{4,0},{8,12},{12,8},{1,5},{5,1},{9,13},{13,9},{2,6},{6,2},{1... | collective-permute-start | bytes 589832 | tf_op jit(solution)/shard_map/ppermute | solution.py:373
  35.1 7.6 %collective-permute-start.5 = (bf16[16,2048]{1,0:T(8,128)(2,1)S(1)}, bf16[16,2048]{1,0:T(8,128)(2,1)S(1)}, u32[]{:S(2)}, u32[]{:S(2)}) collective-permute-start(bf16[16,2048]{1,0:T(8,128)(2,1)S(1)} %shard_map.83.refs_1_), channel_id=1, source_target_pairs={{0,8},{4,12},{8,0},{12,4},{1,9},{5,13},{9,1},{13,5},{2,10},{6,14},... | collective-permute-start | bytes 196616 | tf_op jit(solution)/shard_map/ppermute | solution.py:373
  36.3 6.4 %collective-permute-start.4 = (bf16[16,2048]{1,0:T(8,128)(2,1)S(1)}, bf16[16,2048]{1,0:T(8,128)(2,1)S(1)}, u32[]{:S(2)}, u32[]{:S(2)}) collective-permute-start(bf16[16,2048]{1,0:T(8,128)(2,1)S(1)} %shard_map.83.refs_1_), channel_id=1, source_target_pairs={{0,4},{4,0},{8,12},{12,8},{1,5},{5,1},{9,13},{13,9},{2,6},{6,2},{1... | collective-permute-start | bytes 196616 | tf_op jit(solution)/shard_map/ppermute | solution.py:373
  36.9 7.3 %collective-permute-start.3 = (bf16[16,2048]{1,0:T(8,128)(2,1)S(1)}, bf16[16,2048]{1,0:T(8,128)(2,1)S(1)}, u32[]{:S(2)}, u32[]{:S(2)}) collective-permute-start(bf16[16,2048]{1,0:T(8,128)(2,1)S(1)} %shard_map.83.refs_1_), channel_id=1, source_target_pairs={{0,12},{4,8},{8,4},{12,0},{1,13},{5,9},{9,5},{13,1},{2,14},{6,10},... | collective-permute-start | bytes 196616 | tf_op jit(solution)/shard_map/ppermute | solution.py:373
  45.6 2.0 %collective-permute-start.9 = (f32[2,64,1024]{2,1,0:T(8,128)S(1)}, f32[2,64,1024]{2,1,0:T(8,128)S(1)}, u32[]{:S(2)}, u32[]{:S(2)}) collective-permute-start(f32[2,64,1024]{2,1,0:T(8,128)S(1)} %get-tuple-element.34), channel_id=1, source_target_pairs={{0,1},{1,0},{2,3},{3,2},{4,5},{5,4},{6,7},{7,6},{8,9},{9,8},{10,11... | collective-permute-start | bytes 1572872 | tf_op jit(solution)/shard_map/ppermute | solution.py:410
  47.7 4.1 %collective-permute-start.11 = (bf16[64,1024]{1,0:T(8,128)(2,1)S(1)}, bf16[64,1024]{1,0:T(8,128)(2,1)S(1)}, u32[]{:S(2)}, u32[]{:S(2)}) collective-permute-start(bf16[64,1024]{1,0:T(8,128)(2,1)S(1)} %get-tuple-element.35), channel_id=1, source_target_pairs={{0,8},{1,0},{2,12},{3,4},{4,9},{5,1},{6,13},{7,5},{8,10},{9,2},{10... | collective-permute-start | bytes 393224 | tf_op jit(solution)/shard_map/ppermute | solution.py:418
  47.8 7.7 %collective-permute-start.10 = (bf16[64,1024]{1,0:T(8,128)(2,1)S(1)}, bf16[64,1024]{1,0:T(8,128)(2,1)S(1)}, u32[]{:S(2)}, u32[]{:S(2)}) collective-permute-start(bf16[64,1024]{1,0:T(8,128)(2,1)S(1)} %get-tuple-element.36), channel_id=1, source_target_pairs={{0,12},{1,4},{2,8},{3,0},{4,13},{5,5},{6,9},{7,1},{8,14},{9,6},{10... | collective-permute-start | bytes 393224 | tf_op jit(solution)/shard_map/ppermute | solution.py:418

commit v2 on v1

--- a/solution.py
+++ b/solution.py
@@ -12,6 +12,7 @@
 BLOCK = 128
 LOW = -1e30
 EXTRA = 8
+FLIPS = (0, 1, 3, 2)
 MIX = 3
 
 
@@ -27,14 +28,19 @@
     return pltpu.with_memory_space_constraint(x, pltpu.HBM)
 
 
-def payload_kernel(prompt_ref, blocks_ref, pre_ref, out_ref, sem):
-    keys, kvw = pre_ref.shape[1:]
-    copy = pltpu.make_async_copy(pre_ref, out_ref.at[:, pl.ds(0, keys), :], sem)
-    copy.start()
-    shape = (1, out_ref.shape[1] - keys, kvw // 2)
-    out_ref[:, keys:, : kvw // 2] = jnp.full(shape, prompt_ref[0], jnp.float32).astype(jnp.bfloat16)
-    out_ref[:, keys:, kvw // 2 :] = jnp.full(shape, blocks_ref[0], jnp.float32).astype(jnp.bfloat16)
-    copy.wait()
+def payload_kernel(prompt_ref, blocks_ref, pre_ref, out_ref, sems):
+    _, keys, kvw = pre_ref.shape
+    copies = []
+    for c in range(kvw // HD):
+        source = pre_ref.at[0, :, pl.ds(c * HD, HD)]
+        target = out_ref.at[pl.ds(c * keys, keys), :]
+        copies.append(pltpu.make_async_copy(source, target, sems.at[c]))
+        copies[c].start()
+    lane = lax.broadcasted_iota(jnp.int32, (EXTRA, HD), 1)
+    ids = jnp.where(lane < HD // 2, prompt_ref[0], blocks_ref[0])
+    out_ref[keys * kvw // HD :, :] = ids.astype(jnp.float32).astype(jnp.bfloat16)
+    for copy in copies:
+        copy.wait()
 
 
 def make_payload(prefix_kv, slot_prompt, prefix_blocks):
@@ -42,10 +48,10 @@
     smem = pl.BlockSpec(memory_space=pltpu.SMEM)
     return pl.pallas_call(
         payload_kernel,
-        out_shape=jax.ShapeDtypeStruct((1, keys + EXTRA, kvw), prefix_kv.dtype),
+        out_shape=jax.ShapeDtypeStruct((keys * kvw // HD + EXTRA, HD), prefix_kv.dtype),
         in_specs=[smem, smem, pl.BlockSpec(memory_space=pl.ANY)],
         out_specs=pl.BlockSpec(memory_space=pltpu.VMEM),
-        scratch_shapes=[pltpu.SemaphoreType.DMA],
+        scratch_shapes=[pltpu.SemaphoreType.DMA((kvw // HD,))],
         compiler_params=pltpu.CompilerParams(vmem_limit_bytes=4 << 20),
         name="make_payload",
     )(slot_prompt, prefix_blocks, in_hbm(prefix_kv))
@@ -160,12 +166,10 @@
     )(lengths, in_hbm(queries), in_hbm(fresh), in_hbm(cached))
 
 
-def add_slots_kernel(slots, steps, group, count, *refs):
+def add_slots_kernel(slots, steps, group, heads, count, *refs):
     pre_refs, (q_ref, acc_ref, ml_ref, out_ref, scr) = refs[:count], refs[count:]
     rows = q_ref.shape[0]
-    keys = pre_refs[0].shape[1] - EXTRA
-    kvw = pre_refs[0].shape[2]
-    heads = kvw // (2 * HD)
+    keys = (pre_refs[0].shape[0] - EXTRA) // (2 * heads)
     span = steps * group
     members = rows // slots
     order = range(members)
@@ -173,16 +177,16 @@
     scale = HD ** (-0.5)
     col = lax.broadcasted_iota(jnp.int32, (tall, keys), 1)
     for n, pre_ref in enumerate(pre_refs):
-        extra = pre_ref[0, keys:, :].astype(jnp.float32)
-        prompt = jnp.max(extra[:, :HD]).astype(jnp.int32)
-        length = jnp.max(extra[:, kvw // 2 : kvw // 2 + HD]).astype(jnp.int32) * BLOCK
+        extra = pre_ref[2 * heads * keys :, :].astype(jnp.float32)
+        prompt = jnp.max(extra[:, : HD // 2]).astype(jnp.int32)
+        length = jnp.max(extra[:, HD // 2 :]).astype(jnp.int32) * BLOCK
         for h in range(heads):
-            base = h * 2 * HD
+            base = h * 2 * keys
             at = slice(h * span, (h + 1) * span)
             q = jnp.concatenate([q_ref[prompt + i * slots, at, :] for i in order], axis=0)
             ml = jnp.concatenate([ml_ref[prompt + i * slots, at, :] for i in order], axis=0)
             acc = jnp.concatenate([acc_ref[prompt + i * slots, at, :] for i in order], axis=0)
-            s = nt(q, pre_ref[0, :keys, base : base + HD]) * scale
+            s = nt(q, pre_ref[base : base + keys, :]) * scale
             s = jnp.where(col < length, s, LOW)
             old_top = ml[:, 0:1]
             old_total = ml[:, HD // 2 : HD // 2 + 1]
@@ -190,7 +194,7 @@
             e = jnp.exp(s - top)
             carry = jnp.exp(old_top - top)
             total = jnp.sum(e, axis=1, keepdims=True) + carry * old_total
-            add = nn(e.astype(jnp.bfloat16), pre_ref[0, :keys, base + HD : base + 2 * HD])
+            add = nn(e.astype(jnp.bfloat16), pre_ref[base + keys : base + 2 * keys, :])
             scr[(n * heads + h) * tall : (n * heads + h + 1) * tall, :] = (add + carry * acc) / total
     tile_rows = members * steps
     for n in range(count):
@@ -205,11 +209,11 @@
     rows, per_row, _ = grouped.shape
     group = per_row // (heads * steps)
     count = len(payloads)
-    keys, kvw = payloads[0].shape[1:]
+    keys = (payloads[0].shape[0] - EXTRA) // (2 * heads)
     vmem = pl.BlockSpec(memory_space=pltpu.VMEM)
     shape = (count * rows // slots * steps, heads * group * HD)
     return pl.pallas_call(
-        functools.partial(add_slots_kernel, slots, steps, group, count),
+        functools.partial(add_slots_kernel, slots, steps, group, heads, count),
         out_shape=jax.ShapeDtypeStruct(shape, jnp.bfloat16),
         in_specs=[vmem] * (count + 3),
         out_specs=vmem,
@@ -217,7 +221,7 @@
         compiler_params=pltpu.CompilerParams(vmem_limit_bytes=8 << 20),
         cost_estimate=pl.CostEstimate(
             flops=4 * count * rows * per_row * keys * HD // slots,
-            bytes_accessed=2 * count * keys * kvw,
+            bytes_accessed=4 * count * keys * heads * HD,
             transcendentals=count * rows * per_row * keys // slots,
         ),
     )(*payloads, grouped, acc, ml)
@@ -232,7 +236,7 @@
     came = lax.broadcasted_iota(jnp.int32, (size, size), 1)
     prompt = jnp.zeros((size, size), jnp.int32)
     for k, pre_ref in enumerate(pre_refs):
-        extra = pre_ref[0, pre_ref.shape[1] - EXTRA :, :HD].astype(jnp.float32)
+        extra = pre_ref[pre_ref.shape[0] - EXTRA :, : HD // 2].astype(jnp.float32)
         prompt = jnp.where(came // group == k, jnp.max(extra).astype(jnp.int32), prompt)
     row = prompt + came % group // steps * slots
     hit = place == came % steps * rows + row
@@ -325,18 +329,21 @@
     )(*pieces, weight)
 
 
-def project_last_kernel(blocks, first_homes, homes, pos_ref, *refs):
+def project_last_kernel(blocks, first_homes, homes, *refs):
     parts = len(homes)
+    me, t = lax.axis_index("sample"), lax.axis_index("tensor")
+    mine = (2 * (t % 2) + t // 2) ^ MIX
+    pos = [me ^ flip ^ mine for flip in FLIPS]
     att_refs, (first_ref, w_ref, keep_ref, send_ref, lhs, both) = refs[:parts], refs[parts:]
     at = 0
     for home, start, size in first_homes:
-        both[pos_ref[home], start : start + size, :] = first_ref[at : at + size, :]
+        both[pos[home], start : start + size, :] = first_ref[at : at + size, :]
         at += size
     stack_rows(lhs, att_refs)
     sums = nn(lhs[...], w_ref[...])
     at = 0
     for home, start, size in homes:
-        both[pos_ref[home], start : start + size, :] = sums[at : at + size]
+        both[pos[home], start : start + size, :] = sums[at : at + size]
         at += size
     half = blocks // 2
     for k in range(half):
@@ -344,16 +351,16 @@
         send_ref[k] = both[half + k]
 
 
-def project_last(pieces, homes, first, first_homes, weight, pos, block):
+def project_last(pieces, homes, first, first_homes, weight, block):
     tall = sum(piece.shape[0] for piece in pieces)
-    blocks = pos.shape[0]
+    blocks = len(FLIPS)
     width, cols = weight.shape
     vmem = pl.BlockSpec(memory_space=pltpu.VMEM)
     shape = jax.ShapeDtypeStruct((blocks // 2, block, cols), jnp.float32)
     return pl.pallas_call(
         functools.partial(project_last_kernel, blocks, first_homes, homes),
         out_shape=(shape, shape),
-        in_specs=[pl.BlockSpec(memory_space=pltpu.SMEM)] + [vmem] * (len(pieces) + 2),
+        in_specs=[vmem] * (len(pieces) + 2),
         out_specs=(vmem, vmem),
         scratch_shapes=[
             pltpu.VMEM((tall, width), jnp.bfloat16),
@@ -366,7 +373,7 @@
             transcendentals=0,
         ),
         name="project_last",
-    )(pos, *pieces, first, weight)
+    )(*pieces, first, weight)
 
 
 def exchange(x, size, flip):
@@ -378,10 +385,6 @@
 ):
     steps, rows, _ = queries.shape
     heads = new_kv.shape[2] // (2 * HD)
-    me = lax.axis_index("sample")
-    t = lax.axis_index("tensor")
-    chip, core = t // 2, t % 2
-    flips = (0, 1, 3, 2)
     payload = make_payload(prefix_kv, slot_prompt, prefix_blocks)
     far = exchange(payload, size, 3)
     near = exchange(payload, size, 1)
@@ -405,8 +408,7 @@
     last = [rest_far, rest_near, rest_diag, most_diag]
     homes = ((2, much, little), (1, much, little), (3, much, little), (3, 0, much))
     *last, first = lax.optimization_barrier((*last, first))
-    pos = jnp.stack([me ^ flip for flip in flips]) ^ (2 * core + chip) ^ MIX
-    keep, send = project_last(last, homes, first, first_homes, held, pos, much + little)
+    keep, send = project_last(last, homes, first, first_homes, held, much + little)
     got = lax.ppermute(send, "tensor", [(0, 1), (1, 0), (2, 3), (3, 2)])
     halves = (keep + got).astype(jnp.bfloat16)
     arrived = []

time: 57.1 us -> 61.2 us (1.072)
  waiting for transfers between devices: 15.1 us -> 22.2 us
  starting transfers between devices: 21.5 us -> 19.5 us
    ppermute x9, waiting for transfers between devices: 9.54 us -> 16.6 us  [exchange(): return lax.ppermute(x, 'sample', [(i, i ^ flip) for i in range(size)])]
    ppermute x9, starting transfers between devices: 17.5 us -> 15.5 us  [exchange(): return lax.ppermute(x, 'sample', [(i, i ^ flip) for i in range(size)])]
  transfers between devices with their start and end apart: 12 -> 12, of which waited for: 5 -> 7; matrix products, arithmetic and copies ran while one was open for 0% -> 0% of each run, Pallas kernels for 25% -> 19%
where the time goes in v2:
time: 61.2 us; the launch traced here: 60.7 us
  waiting for transfers between devices  22.2 us (36%)
  starting transfers between devices  19.5 us (32%)
  Pallas kernels  16.9 us (28%)
  between operations  1.43 us (2%)
  local copies, waits for them, and re-layouts  0.67 us (1%)
    ppermute x9, waiting for transfers between devices, exchange(): return lax.ppermute(x, 'sample', [(i, i ^ flip) for i in range(size)])  16.6 us
    ppermute x9, starting transfers between devices, exchange(): return lax.ppermute(x, 'sample', [(i, i ^ flip) for i in range(size)])  15.5 us
    pallas_call x1, Pallas kernels, gen_attention(): pl.pallas_call(functools.partial(gen_kernel, steps, heads, group), out_sh...  7.5 us
    ppermute x2, starting transfers between devices, direct(): piece = lax.ppermute(halves[i], ('sample', 'tensor'), perm)  3.95 us
    ppermute x2, waiting for transfers between devices, direct(): piece = lax.ppermute(halves[i], ('sample', 'tensor'), perm)  3.65 us
    pallas_call x2, Pallas kernels, add_slots(): pl.pallas_call(functools.partial(add_slots_kernel, slots, steps, group, h...  3.49 us
    pallas_call x1, Pallas kernels, hold(): pl.pallas_call(hold_kernel, out_shape=jax.ShapeDtypeStruct(weight.shape,...  2.2 us
    ppermute x1, waiting for transfers between devices, direct(): got = lax.ppermute(send, 'tensor', [(0, 1), (1, 0), (2, 3), (3, 2)])  1.9 us
  transfers between devices with their start and end apart: 12, of which 7 were waited for; matrix products, arithmetic and copies ran while one was open for 0% of the time, Pallas kernels for 19%

profile of v2, /device:TPU:0, one launch (start us, length us, event | category | flops | bytes accessed | tf_op | source)
XLA Modules:
  0.0 60.7 jit_solution(17462400086432216268)
XLA Ops:
  1.3 1.0 %make_payload.1.refs_0_ = bf16[1032,128]{1,0:T(8,128)(2,1)S(1)} custom-call(s32[1]{0:T(128)S(6)} %copy.9.prompt_ref, s32[1]{0:T(128)S(6)} %copy.10.blocks_ref, bf16[1,256,512]{2,1,0:T(8,128)(2,1)} %pre_ref.1), custom_call_target="tpu_custom_call" | custom-call | tf_op jit(solution)/shard_map/make_payload/pallas_call | solution.py:49
  2.3 5.1 %collective-permute-start.1 = (bf16[1032,128]{1,0:T(8,128)(2,1)S(1)}, bf16[1032,128]{1,0:T(8,128)(2,1)S(1)}, u32[]{:S(2)}, u32[]{:S(2)}) collective-permute-start(bf16[1032,128]{1,0:T(8,128)(2,1)S(1)} %make_payload.1.refs_0_), channel_id=1, source_target_pairs={{0,12},{4,8},{8,4},{12,0},{1,13},{5,9},{9,5},{13,1},{2,14},{6,10},... | collective-permute-start | bytes 792584 | tf_op jit(solution)/shard_map/ppermute | solution.py:380
  7.4 0.7 %copy-done = s32[16]{0:T(128)S(1)} copy-done((s32[16]{0:T(128)S(1)}, s32[16]{0:T(128)}, u32[]{:S(2)}) %copy-start) | copy-done | bytes 88
  8.1 7.5 %gen_attention.1 = (bf16[16,64,128]{2,1,0:T(8,128)(2,1)S(1)}, f32[16,64,128]{2,1,0:T(8,128)S(1)}, f32[16,64,128]{2,1,0:T(8,128)S(1)}) custom-call(s32[16]{0:T(128)S(1)} %copy-done, bf16[4,16,2048]{2,1,0:T(8,128)(2,1)} %q_ref.1, bf16[4,16,512]{2,1,0:T(8,128)(2,1)} %new_ref.1, bf16[16,512,512]{2,1,0:T(8,128)(2,1)} %kv_ref.1), custom_call_target="tpu_custom_call" | custom-call | flops 268435456 | bytes 8388608 | tf_op jit(solution)/shard_map/gen_attention/pallas_call | solution.py:137
  15.6 3.9 %collective-permute-done.refs_1_ = bf16[1032,128]{1,0:T(8,128)(2,1)S(1)} collective-permute-done((bf16[1032,128]{1,0:T(8,128)(2,1)S(1)}, bf16[1032,128]{1,0:T(8,128)(2,1)S(1)}, u32[]{:S(2)}, u32[]{:S(2)}) %collective-permute-start) | collective-permute-done | bytes 264224 | tf_op jit(solution)/shard_map/ppermute | solution.py:380
  19.5 2.6 %shard_map.82.refs_0_ = bf16[48,2048]{1,0:T(8,128)(2,1)S(1)} custom-call(bf16[1032,128]{1,0:T(8,128)(2,1)S(1)} %make_payload.1.refs_0_, bf16[1032,128]{1,0:T(8,128)(2,1)S(1)} %collective-permute-done.refs_1_, bf16[1032,128]{1,0:T(8,128)(2,1)S(1)} %collective-permute-done.1.refs_2_, bf16[16,64,128]{2,1,0:T(8,128)(2,1)S(1)} %get-tuple-element.24.refs_3_.refs_1_, ...), custom_call_target="tpu_custom_call" | custom-call | flops 100663296 | bytes 786432 | tf_op jit(solution)/shard_map/pallas_call | solution.py:215
  22.1 1.8 %collective-permute-start.6 = (bf16[48,2048]{1,0:T(8,128)(2,1)S(1)}, bf16[48,2048]{1,0:T(8,128)(2,1)S(1)}, u32[]{:S(2)}, u32[]{:S(2)}) collective-permute-start(bf16[48,2048]{1,0:T(8,128)(2,1)S(1)} %shard_map.82.refs_0_), channel_id=1, source_target_pairs={{0,12},{4,8},{8,4},{12,0},{1,13},{5,9},{9,5},{13,1},{2,14},{6,10},... | collective-permute-start | bytes 589832 | tf_op jit(solution)/shard_map/ppermute | solution.py:380
  24.0 2.0 %collective-permute-start.8 = (bf16[48,2048]{1,0:T(8,128)(2,1)S(1)}, bf16[48,2048]{1,0:T(8,128)(2,1)S(1)}, u32[]{:S(2)}, u32[]{:S(2)}) collective-permute-start(bf16[48,2048]{1,0:T(8,128)(2,1)S(1)} %shard_map.82.refs_0_), channel_id=1, source_target_pairs={{0,4},{4,0},{8,12},{12,8},{1,5},{5,1},{9,13},{13,9},{2,6},{6,2},{1... | collective-permute-start | bytes 589832 | tf_op jit(solution)/shard_map/ppermute | solution.py:380
  25.9 5.9 %collective-permute-done.6.refs_2_ = bf16[48,2048]{1,0:T(8,128)(2,1)S(1)} collective-permute-done((bf16[48,2048]{1,0:T(8,128)(2,1)S(1)}, bf16[48,2048]{1,0:T(8,128)(2,1)S(1)}, u32[]{:S(2)}, u32[]{:S(2)}) %collective-permute-start.6) | collective-permute-done | bytes 196640 | tf_op jit(solution)/shard_map/ppermute | solution.py:380
  31.8 2.1 %collective-permute-start.7 = (bf16[48,2048]{1,0:T(8,128)(2,1)S(1)}, bf16[48,2048]{1,0:T(8,128)(2,1)S(1)}, u32[]{:S(2)}, u32[]{:S(2)}) collective-permute-start(bf16[48,2048]{1,0:T(8,128)(2,1)S(1)} %collective-permute-done.6.refs_2_), channel_id=1, source_target_pairs={{0,4},{4,0},{8,12},{12,8},{1,5},{5,1},{9,13},{13,9},{2,6},{6,2},{1... | collective-permute-start | bytes 589832 | tf_op jit(solution)/shard_map/ppermute | solution.py:380
  33.9 2.7 %collective-permute-done.2.refs_3_.refs_0_ = bf16[1032,128]{1,0:T(8,128)(2,1)S(1)} collective-permute-done((bf16[1032,128]{1,0:T(8,128)(2,1)S(1)}, bf16[1032,128]{1,0:T(8,128)(2,1)S(1)}, u32[]{:S(2)}, u32[]{:S(2)}) %collective-permute-start.2) | collective-permute-done | bytes 264224 | tf_op jit(solution)/shard_map/ppermute | solution.py:380
  36.6 0.9 %shard_map.83.refs_1_ = bf16[16,2048]{1,0:T(8,128)(2,1)S(1)} custom-call(bf16[1032,128]{1,0:T(8,128)(2,1)S(1)} %collective-permute-done.2.refs_3_.refs_0_, bf16[16,64,128]{2,1,0:T(8,128)(2,1)S(1)} %get-tuple-element.24.refs_3_.refs_1_, f32[16,64,128]{2,1,0:T(8,128)S(1)} %get-tuple-element.25.refs_4_.refs_2_, f32[16,64,128]{2,1,0:T(8,128)S(1)} %get-tuple-element.26.refs_5_.refs_3_), custom_call_target="tpu_custom_call" | custom-call | flops 33554432 | bytes 262144 | tf_op jit(solution)/shard_map/pallas_call | solution.py:215
  37.5 1.5 %collective-permute-start.5 = (bf16[16,2048]{1,0:T(8,128)(2,1)S(1)}, bf16[16,2048]{1,0:T(8,128)(2,1)S(1)}, u32[]{:S(2)}, u32[]{:S(2)}) collective-permute-start(bf16[16,2048]{1,0:T(8,128)(2,1)S(1)} %shard_map.83.refs_1_), channel_id=1, source_target_pairs={{0,8},{4,12},{8,0},{12,4},{1,9},{5,13},{9,1},{13,5},{2,10},{6,14},... | collective-permute-start | bytes 196616 | tf_op jit(solution)/shard_map/ppermute | solution.py:380
  39.0 2.9 %collective-permute-start.3 = (bf16[16,2048]{1,0:T(8,128)(2,1)S(1)}, bf16[16,2048]{1,0:T(8,128)(2,1)S(1)}, u32[]{:S(2)}, u32[]{:S(2)}) collective-permute-start(bf16[16,2048]{1,0:T(8,128)(2,1)S(1)} %shard_map.83.refs_1_), channel_id=1, source_target_pairs={{0,12},{4,8},{8,4},{12,0},{1,13},{5,9},{9,5},{13,1},{2,14},{6,10},... | collective-permute-start | bytes 196616 | tf_op jit(solution)/shard_map/ppermute | solution.py:380
  41.9 2.2 %hold.1.refs_4_.refs_5_ = bf16[2048,1024]{1,0:T(8,128)(2,1)S(1)} custom-call(bf16[2048,1024]{1,0:T(8,128)(2,1)} %w_ref.1), custom_call_target="tpu_custom_call" | custom-call | tf_op jit(solution)/shard_map/hold/pallas_call | solution.py:287
  44.2 0.8 %project_first.1.refs_4_ = f32[160,1024]{1,0:T(8,128)S(1)} custom-call(bf16[48,2048]{1,0:T(8,128)(2,1)S(1)} %shard_map.82.refs_0_, bf16[16,2048]{1,0:T(8,128)(2,1)S(1)} %shard_map.83.refs_1_, bf16[48,2048]{1,0:T(8,128)(2,1)S(1)} %collective-permute-done.6.refs_2_, bf16[48,2048]{1,0:T(8,128)(2,1)S(1)} %collective-permute-done.8.refs_3_, ...), custom_call_target="tpu_custom_call" | custom-call | flops 671088640 | bytes 4194304 | tf_op jit(solution)/shard_map/project_first/pallas_call | solution.py:316
  45.0 1.3 %collective-permute-done.4.refs_1_ = bf16[16,2048]{1,0:T(8,128)(2,1)S(1)} collective-permute-done((bf16[16,2048]{1,0:T(8,128)(2,1)S(1)}, bf16[16,2048]{1,0:T(8,128)(2,1)S(1)}, u32[]{:S(2)}, u32[]{:S(2)}) %collective-permute-start.4) | collective-permute-done | bytes 65568 | tf_op jit(solution)/shard_map/ppermute | solution.py:380
  46.3 2.8 %collective-permute-done.3.refs_0_ = bf16[16,2048]{1,0:T(8,128)(2,1)S(1)} collective-permute-done((bf16[16,2048]{1,0:T(8,128)(2,1)S(1)}, bf16[16,2048]{1,0:T(8,128)(2,1)S(1)}, u32[]{:S(2)}, u32[]{:S(2)}) %collective-permute-start.3) | collective-permute-done | bytes 65568 | tf_op jit(solution)/shard_map/ppermute | solution.py:380
  49.2 0.9 %project_last.1 = (f32[2,64,1024]{2,1,0:T(8,128)S(1)}, f32[2,64,1024]{2,1,0:T(8,128)S(1)}) custom-call(bf16[16,2048]{1,0:T(8,128)(2,1)S(1)} %collective-permute-done.3.refs_0_, bf16[16,2048]{1,0:T(8,128)(2,1)S(1)} %collective-permute-done.4.refs_1_, bf16[16,2048]{1,0:T(8,128)(2,1)S(1)} %collective-permute-done.5.refs_2_, ...), custom_call_target="tpu_custom_call" | custom-call | flops 402653184 | bytes 4194304 | tf_op jit(solution)/shard_map/project_last/pallas_call | solution.py:360
  50.1 1.9 %collective-permute-done.9 = f32[2,64,1024]{2,1,0:T(8,128)S(1)} collective-permute-done((f32[2,64,1024]{2,1,0:T(8,128)S(1)}, f32[2,64,1024]{2,1,0:T(8,128)S(1)}, u32[]{:S(2)}, u32[]{:S(2)}) %collective-permute-start.9) | collective-permute-done | bytes 524320 | tf_op jit(solution)/shard_map/ppermute | solution.py:412
  52.2 3.9 %collective-permute-start.10 = (bf16[64,1024]{1,0:T(8,128)(2,1)S(1)}, bf16[64,1024]{1,0:T(8,128)(2,1)S(1)}, u32[]{:S(2)}, u32[]{:S(2)}) collective-permute-start(bf16[64,1024]{1,0:T(8,128)(2,1)S(1)} %get-tuple-element.36), channel_id=1, source_target_pairs={{0,12},{1,4},{2,8},{3,0},{4,13},{5,5},{6,9},{7,1},{8,14},{9,6},{10... | collective-permute-start | bytes 393224 | tf_op jit(solution)/shard_map/ppermute | solution.py:420
  56.1 0.1 row_order.1.order_ref
  56.2 3.6 %collective-permute-done.10.a_ref = bf16[64,1024]{1,0:T(8,128)(2,1)S(1)} collective-permute-done((bf16[64,1024]{1,0:T(8,128)(2,1)S(1)}, bf16[64,1024]{1,0:T(8,128)(2,1)S(1)}, u32[]{:S(2)}, u32[]{:S(2)}) %collective-permute-start.10) | collective-permute-done | bytes 131104 | tf_op jit(solution)/shard_map/ppermute | solution.py:420
  59.9 0.8 %finish.1 = bf16[64,1024]{1,0:T(8,128)(2,1)} custom-call(bf16[64,64]{1,0:T(8,128)(2,1)S(1)} %row_order.1.order_ref, bf16[64,1024]{1,0:T(8,128)(2,1)S(1)} %collective-permute-done.10.a_ref, bf16[64,1024]{1,0:T(8,128)(2,1)S(1)} %collective-permute-done.11.b_ref), custom_call_target="tpu_custom_call" | custom-call | tf_op jit(solution)/shard_map/finish/pallas_call | solution.py:265
  (13 shorter events, 0.3 us)
Async XLA Ops:
  2.3 13.3 %collective-permute-start.1 = (bf16[1032,128]{1,0:T(8,128)(2,1)S(1)}, bf16[1032,128]{1,0:T(8,128)(2,1)S(1)}, u32[]{:S(2)}, u32[]{:S(2)}) collective-permute-start(bf16[1032,128]{1,0:T(8,128)(2,1)S(1)} %make_payload.1.refs_0_), channel_id=1, source_target_pairs={{0,12},{4,8},{8,4},{12,0},{1,13},{5,9},{9,5},{13,1},{2,14},{6,10},... | collective-permute-start | bytes 792584 | tf_op jit(solution)/shard_map/ppermute | solution.py:380
  7.4 12.1 %collective-permute-start = (bf16[1032,128]{1,0:T(8,128)(2,1)S(1)}, bf16[1032,128]{1,0:T(8,128)(2,1)S(1)}, u32[]{:S(2)}, u32[]{:S(2)}) collective-permute-start(bf16[1032,128]{1,0:T(8,128)(2,1)S(1)} %make_payload.1.refs_0_), channel_id=1, source_target_pairs={{0,4},{4,0},{8,12},{12,8},{1,5},{5,1},{9,13},{13,9},{2,6},{6,2},{1... | collective-permute-start | bytes 792584 | tf_op jit(solution)/shard_map/ppermute | solution.py:380
  7.4 0.7 %copy-start = (s32[16]{0:T(128)S(1)}, s32[16]{0:T(128)}, u32[]{:S(2)}) copy-start(s32[16]{0:T(128)} %len_ref.1) | copy-start | bytes 196
  22.1 9.7 %collective-permute-start.6 = (bf16[48,2048]{1,0:T(8,128)(2,1)S(1)}, bf16[48,2048]{1,0:T(8,128)(2,1)S(1)}, u32[]{:S(2)}, u32[]{:S(2)}) collective-permute-start(bf16[48,2048]{1,0:T(8,128)(2,1)S(1)} %shard_map.82.refs_0_), channel_id=1, source_target_pairs={{0,12},{4,8},{8,4},{12,0},{1,13},{5,9},{9,5},{13,1},{2,14},{6,10},... | collective-permute-start | bytes 589832 | tf_op jit(solution)/shard_map/ppermute | solution.py:380
  23.9 12.7 %collective-permute-start.2 = (bf16[1032,128]{1,0:T(8,128)(2,1)S(1)}, bf16[1032,128]{1,0:T(8,128)(2,1)S(1)}, u32[]{:S(2)}, u32[]{:S(2)}) collective-permute-start(bf16[1032,128]{1,0:T(8,128)(2,1)S(1)} %collective-permute-done.1.refs_2_), channel_id=1, source_target_pairs={{0,4},{4,0},{8,12},{12,8},{1,5},{5,1},{9,13},{13,9},{2,6},{6,2},{1... | collective-permute-start | bytes 792584 | tf_op jit(solution)/shard_map/ppermute | solution.py:380
  24.0 20.2 %collective-permute-start.8 = (bf16[48,2048]{1,0:T(8,128)(2,1)S(1)}, bf16[48,2048]{1,0:T(8,128)(2,1)S(1)}, u32[]{:S(2)}, u32[]{:S(2)}) collective-permute-start(bf16[48,2048]{1,0:T(8,128)(2,1)S(1)} %shard_map.82.refs_0_), channel_id=1, source_target_pairs={{0,4},{4,0},{8,12},{12,8},{1,5},{5,1},{9,13},{13,9},{2,6},{6,2},{1... | collective-permute-start | bytes 589832 | tf_op jit(solution)/shard_map/ppermute | solution.py:380
  31.8 17.3 %collective-permute-start.7 = (bf16[48,2048]{1,0:T(8,128)(2,1)S(1)}, bf16[48,2048]{1,0:T(8,128)(2,1)S(1)}, u32[]{:S(2)}, u32[]{:S(2)}) collective-permute-start(bf16[48,2048]{1,0:T(8,128)(2,1)S(1)} %collective-permute-done.6.refs_2_), channel_id=1, source_target_pairs={{0,4},{4,0},{8,12},{12,8},{1,5},{5,1},{9,13},{13,9},{2,6},{6,2},{1... | collective-permute-start | bytes 589832 | tf_op jit(solution)/shard_map/ppermute | solution.py:380
  37.5 7.5 %collective-permute-start.5 = (bf16[16,2048]{1,0:T(8,128)(2,1)S(1)}, bf16[16,2048]{1,0:T(8,128)(2,1)S(1)}, u32[]{:S(2)}, u32[]{:S(2)}) collective-permute-start(bf16[16,2048]{1,0:T(8,128)(2,1)S(1)} %shard_map.83.refs_1_), channel_id=1, source_target_pairs={{0,8},{4,12},{8,0},{12,4},{1,9},{5,13},{9,1},{13,5},{2,10},{6,14},... | collective-permute-start | bytes 196616 | tf_op jit(solution)/shard_map/ppermute | solution.py:380
  39.0 7.3 %collective-permute-start.4 = (bf16[16,2048]{1,0:T(8,128)(2,1)S(1)}, bf16[16,2048]{1,0:T(8,128)(2,1)S(1)}, u32[]{:S(2)}, u32[]{:S(2)}) collective-permute-start(bf16[16,2048]{1,0:T(8,128)(2,1)S(1)} %shard_map.83.refs_1_), channel_id=1, source_target_pairs={{0,4},{4,0},{8,12},{12,8},{1,5},{5,1},{9,13},{13,9},{2,6},{6,2},{1... | collective-permute-start | bytes 196616 | tf_op jit(solution)/shard_map/ppermute | solution.py:380
  39.0 10.2 %collective-permute-start.3 = (bf16[16,2048]{1,0:T(8,128)(2,1)S(1)}, bf16[16,2048]{1,0:T(8,128)(2,1)S(1)}, u32[]{:S(2)}, u32[]{:S(2)}) collective-permute-start(bf16[16,2048]{1,0:T(8,128)(2,1)S(1)} %shard_map.83.refs_1_), channel_id=1, source_target_pairs={{0,12},{4,8},{8,4},{12,0},{1,13},{5,9},{9,5},{13,1},{2,14},{6,10},... | collective-permute-start | bytes 196616 | tf_op jit(solution)/shard_map/ppermute | solution.py:380
  50.1 2.0 %collective-permute-start.9 = (f32[2,64,1024]{2,1,0:T(8,128)S(1)}, f32[2,64,1024]{2,1,0:T(8,128)S(1)}, u32[]{:S(2)}, u32[]{:S(2)}) collective-permute-start(f32[2,64,1024]{2,1,0:T(8,128)S(1)} %get-tuple-element.34), channel_id=1, source_target_pairs={{0,1},{1,0},{2,3},{3,2},{4,5},{5,4},{6,7},{7,6},{8,9},{9,8},{10,11... | collective-permute-start | bytes 1572872 | tf_op jit(solution)/shard_map/ppermute | solution.py:412
  52.1 4.1 %collective-permute-start.11 = (bf16[64,1024]{1,0:T(8,128)(2,1)S(1)}, bf16[64,1024]{1,0:T(8,128)(2,1)S(1)}, u32[]{:S(2)}, u32[]{:S(2)}) collective-permute-start(bf16[64,1024]{1,0:T(8,128)(2,1)S(1)} %get-tuple-element.35), channel_id=1, source_target_pairs={{0,8},{1,0},{2,12},{3,4},{4,9},{5,1},{6,13},{7,5},{8,10},{9,2},{10... | collective-permute-start | bytes 393224 | tf_op jit(solution)/shard_map/ppermute | solution.py:420
  52.2 7.7 %collective-permute-start.10 = (bf16[64,1024]{1,0:T(8,128)(2,1)S(1)}, bf16[64,1024]{1,0:T(8,128)(2,1)S(1)}, u32[]{:S(2)}, u32[]{:S(2)}) collective-permute-start(bf16[64,1024]{1,0:T(8,128)(2,1)S(1)} %get-tuple-element.36), channel_id=1, source_target_pairs={{0,12},{1,4},{2,8},{3,0},{4,13},{5,5},{6,9},{7,1},{8,14},{9,6},{10... | collective-permute-start | bytes 393224 | tf_op jit(solution)/shard_map/ppermute | solution.py:420

commit v3 on v2

--- a/solution.py
+++ b/solution.py
@@ -28,14 +28,19 @@
     return pltpu.with_memory_space_constraint(x, pltpu.HBM)
 
 
-def payload_kernel(prompt_ref, blocks_ref, pre_ref, out_ref, sems):
+def payload_kernel(prompt_ref, blocks_ref, pre_ref, out_ref, part_ref, sems):
     _, keys, kvw = pre_ref.shape
     copies = []
     for c in range(kvw // HD):
         source = pre_ref.at[0, :, pl.ds(c * HD, HD)]
         target = out_ref.at[pl.ds(c * keys, keys), :]
-        copies.append(pltpu.make_async_copy(source, target, sems.at[c]))
-        copies[c].start()
+        copies.append(pltpu.make_async_copy(source, target, sems.at[0, c]))
+        copies[-1].start()
+    for c in range(kvw // HD // 2):
+        source = pre_ref.at[0, :, pl.ds(c * HD, HD)]
+        target = part_ref.at[pl.ds(c * keys, keys), :]
+        copies.append(pltpu.make_async_copy(source, target, sems.at[1, c]))
+        copies[-1].start()
     lane = lax.broadcasted_iota(jnp.int32, (EXTRA, HD), 1)
     ids = jnp.where(lane < HD // 2, prompt_ref[0], blocks_ref[0])
     out_ref[keys * kvw // HD :, :] = ids.astype(jnp.float32).astype(jnp.bfloat16)
@@ -48,10 +53,13 @@
     smem = pl.BlockSpec(memory_space=pltpu.SMEM)
     return pl.pallas_call(
         payload_kernel,
-        out_shape=jax.ShapeDtypeStruct((keys * kvw // HD + EXTRA, HD), prefix_kv.dtype),
+        out_shape=(
+            jax.ShapeDtypeStruct((keys * kvw // HD + EXTRA, HD), prefix_kv.dtype),
+            jax.ShapeDtypeStruct((keys * kvw // HD // 2, HD), prefix_kv.dtype),
+        ),
         in_specs=[smem, smem, pl.BlockSpec(memory_space=pl.ANY)],
-        out_specs=pl.BlockSpec(memory_space=pltpu.VMEM),
-        scratch_shapes=[pltpu.SemaphoreType.DMA((kvw // HD,))],
+        out_specs=[pl.BlockSpec(memory_space=pltpu.VMEM)] * 2,
+        scratch_shapes=[pltpu.SemaphoreType.DMA((2, kvw // HD))],
         compiler_params=pltpu.CompilerParams(vmem_limit_bytes=4 << 20),
         name="make_payload",
     )(slot_prompt, prefix_blocks, in_hbm(prefix_kv))
@@ -166,22 +174,23 @@
     )(lengths, in_hbm(queries), in_hbm(fresh), in_hbm(cached))
 
 
-def add_slots_kernel(slots, steps, group, heads, count, *refs):
-    pre_refs, (q_ref, acc_ref, ml_ref, out_ref, scr) = refs[:count], refs[count:]
+def add_slots_kernel(slots, steps, group, heads, parts, keys, *refs):
+    (q_ref, acc_ref, ml_ref, out_ref, scr), count = refs[sum(parts) :], len(parts)
     rows = q_ref.shape[0]
-    keys = (pre_refs[0].shape[0] - EXTRA) // (2 * heads)
     span = steps * group
     members = rows // slots
     order = range(members)
     tall = members * span
     scale = HD ** (-0.5)
     col = lax.broadcasted_iota(jnp.int32, (tall, keys), 1)
-    for n, pre_ref in enumerate(pre_refs):
-        extra = pre_ref[2 * heads * keys :, :].astype(jnp.float32)
+    for n in range(count):
+        pre_refs = refs[sum(parts[:n]) : sum(parts[: n + 1])]
+        extra = pre_refs[-1][pre_refs[-1].shape[0] - EXTRA :, :].astype(jnp.float32)
         prompt = jnp.max(extra[:, : HD // 2]).astype(jnp.int32)
         length = jnp.max(extra[:, HD // 2 :]).astype(jnp.int32) * BLOCK
         for h in range(heads):
-            base = h * 2 * keys
+            pre_ref = pre_refs[h * parts[n] // heads]
+            base = h % (heads // parts[n]) * 2 * keys
             at = slice(h * span, (h + 1) * span)
             q = jnp.concatenate([q_ref[prompt + i * slots, at, :] for i in order], axis=0)
             ml = jnp.concatenate([ml_ref[prompt + i * slots, at, :] for i in order], axis=0)
@@ -205,17 +214,17 @@
                 out_ref[n * tile_rows : (n + 1) * tile_rows, cols] = tile.astype(jnp.bfloat16)
 
 
-def add_slots(grouped, acc, ml, payloads, slots, steps, heads):
+def add_slots(grouped, acc, ml, payloads, slots, steps, heads, keys):
     rows, per_row, _ = grouped.shape
     group = per_row // (heads * steps)
     count = len(payloads)
-    keys = (payloads[0].shape[0] - EXTRA) // (2 * heads)
+    parts = [len(payload) for payload in payloads]
     vmem = pl.BlockSpec(memory_space=pltpu.VMEM)
     shape = (count * rows // slots * steps, heads * group * HD)
     return pl.pallas_call(
-        functools.partial(add_slots_kernel, slots, steps, group, heads, count),
+        functools.partial(add_slots_kernel, slots, steps, group, heads, parts, keys),
         out_shape=jax.ShapeDtypeStruct(shape, jnp.bfloat16),
-        in_specs=[vmem] * (count + 3),
+        in_specs=[vmem] * (sum(parts) + 3),
         out_specs=vmem,
         scratch_shapes=[pltpu.VMEM((count * rows // slots * per_row, HD), jnp.float32)],
         compiler_params=pltpu.CompilerParams(vmem_limit_bytes=8 << 20),
@@ -224,7 +233,7 @@
             bytes_accessed=4 * count * keys * heads * HD,
             transcendentals=count * rows * per_row * keys // slots,
         ),
-    )(*payloads, grouped, acc, ml)
+    )(*sum(payloads, []), grouped, acc, ml)
 
 
 def order_kernel(steps, rows, *refs):
@@ -385,22 +394,24 @@
 ):
     steps, rows, _ = queries.shape
     heads = new_kv.shape[2] // (2 * HD)
-    payload = make_payload(prefix_kv, slot_prompt, prefix_blocks)
+    payload, part = make_payload(prefix_kv, slot_prompt, prefix_blocks)
+    keys = prefix_kv.shape[1]
     far = exchange(payload, size, 3)
     near = exchange(payload, size, 1)
+    direct_half = exchange(part, size, 2)
     grouped, acc, ml = gen_attention(queries, new_kv, gen_kv, gen_len, heads, 4)
     far, grouped, acc, ml = lax.optimization_barrier((far, grouped, acc, ml))
-    diag = exchange(far, size, 1)
-    most = add_slots(grouped, acc, ml, [payload, near, far], size, steps, heads)
+    diag = exchange(far[part.shape[0] :], size, 1)
+    most = add_slots(grouped, acc, ml, [[payload], [far]], size, steps, heads, keys)
     most_far = exchange(most, size, 3)
     most_near = exchange(most, size, 1)
-    diag, _ = lax.optimization_barrier((diag, most))
-    rest = add_slots(grouped, acc, ml, [diag], size, steps, heads)
+    near, direct_half, diag, _ = lax.optimization_barrier((near, direct_half, diag, most))
+    rest = add_slots(grouped, acc, ml, [[near], [direct_half, diag]], size, steps, heads, keys)
     rest_far = exchange(rest, size, 3)
     rest_near = exchange(rest, size, 1)
     most_diag = exchange(most_far, size, 1)
     rest_diag = exchange(rest, size, 2)
-    order = row_order([payload, near, far, diag], steps, rows)
+    order = row_order([payload, far, near, diag], steps, rows)
     much, little = most.shape[0], rest.shape[0]
     held = hold(out_weight)
     first = project_first([most, rest, most_far, most_near], held)
@@ -483,6 +494,7 @@
 def shards(queries, new_kv, gen_kv, prefix_kv, slot_prompt, prefix_blocks, gen_len, out_weight):
     size = lax.axis_size("sample")
     fits = size == 4 and lax.axis_size("tensor") == 4 and prefix_kv.shape[0] == 1
+    fits = fits and new_kv.shape[2] % (4 * HD) == 0
     if fits and queries.shape[0] * queries.shape[1] % (16 * size) == 0:
         return direct(
             queries, new_kv, gen_kv, prefix_kv, slot_prompt, prefix_blocks, gen_len, out_weight, size

time: 61.2 us -> 61 us (level)
  starting transfers between devices: 19.5 us -> 27.4 us
  waiting for transfers between devices: 22.2 us -> 14.6 us
  Pallas kernels: 16.9 us -> 16.1 us
    ppermute x9 -> x10, waiting for transfers between devices: 16.6 us -> 10.1 us  [exchange(): return lax.ppermute(x, 'sample', [(i, i ^ flip) for i in range(size)])]
    ppermute x9 -> x10, starting transfers between devices: 15.5 us -> 20.2 us  [exchange(): return lax.ppermute(x, 'sample', [(i, i ^ flip) for i in range(size)])]
    ppermute x2, starting transfers between devices: 3.95 us -> 7.17 us  [direct(): piece = lax.ppermute(halves[i], ('sample', 'tensor'), perm)]
    ppermute x2, waiting for transfers between devices: 3.65 us -> 2.56 us  [direct(): piece = lax.ppermute(halves[i], ('sample', 'tensor'), perm)]
    pallas_call x2, Pallas kernels: 3.49 us -> 2.8 us  [add_slots(): pl.pallas_call(functools.partial(add_slots_kernel, slots, steps, group, h...]
  transfers between devices with their start and end apart: 12 -> 13, of which waited for: 7 -> 5; matrix products, arithmetic and copies ran while one was open for 0% -> 0% of each run, Pallas kernels for 19% -> 22%
where the time goes in v3:
time: 61 us; the launch traced here: 60.2 us
  starting transfers between devices  27.4 us (45%)
  Pallas kernels  16.1 us (26%)
  waiting for transfers between devices  14.6 us (24%)
  between operations  1.42 us (2%)
  local copies, waits for them, and re-layouts  0.69 us (1%)
    ppermute x10, starting transfers between devices, exchange(): return lax.ppermute(x, 'sample', [(i, i ^ flip) for i in range(size)])  20.2 us
    ppermute x10, waiting for transfers between devices, exchange(): return lax.ppermute(x, 'sample', [(i, i ^ flip) for i in range(size)])  10.1 us
    pallas_call x1, Pallas kernels, gen_attention(): pl.pallas_call(functools.partial(gen_kernel, steps, heads, group), out_sh...  7.5 us
    ppermute x2, starting transfers between devices, direct(): piece = lax.ppermute(halves[i], ('sample', 'tensor'), perm)  7.17 us
    pallas_call x2, Pallas kernels, add_slots(): pl.pallas_call(functools.partial(add_slots_kernel, slots, steps, group, h...  2.8 us
    ppermute x2, waiting for transfers between devices, direct(): piece = lax.ppermute(halves[i], ('sample', 'tensor'), perm)  2.56 us
    pallas_call x1, Pallas kernels, hold(): pl.pallas_call(hold_kernel, out_shape=jax.ShapeDtypeStruct(weight.shape,...  2.2 us
    ppermute x1, waiting for transfers between devices, direct(): got = lax.ppermute(send, 'tensor', [(0, 1), (1, 0), (2, 3), (3, 2)])  1.9 us
  transfers between devices with their start and end apart: 13, of which 5 were waited for; matrix products, arithmetic and copies ran while one was open for 0% of the time, Pallas kernels for 22%

profile of v3, /device:TPU:0, one launch (start us, length us, event | category | flops | bytes accessed | tf_op | source)
XLA Modules:
  0.0 60.2 jit_solution(14290679968963175866)
XLA Ops:
  1.3 1.1 %make_payload.1 = (bf16[1032,128]{1,0:T(8,128)(2,1)S(1)}, bf16[512,128]{1,0:T(8,128)(2,1)S(1)}) custom-call(s32[1]{0:T(128)S(6)} %copy.9.prompt_ref, s32[1]{0:T(128)S(6)} %copy.10.blocks_ref, bf16[1,256,512]{2,1,0:T(8,128)(2,1)} %pre_ref.1), custom_call_target="tpu_custom_call" | custom-call | tf_op jit(solution)/shard_map/make_payload/pallas_call | solution.py:54
  2.4 5.1 %collective-permute-start = (bf16[1032,128]{1,0:T(8,128)(2,1)S(1)}, bf16[1032,128]{1,0:T(8,128)(2,1)S(1)}, u32[]{:S(2)}, u32[]{:S(2)}) collective-permute-start(bf16[1032,128]{1,0:T(8,128)(2,1)S(1)} %get-tuple-element.24.refs_0_), channel_id=1, source_target_pairs={{0,12},{4,8},{8,4},{12,0},{1,13},{5,9},{9,5},{13,1},{2,14},{6,10},... | collective-permute-start | bytes 792584 | tf_op jit(solution)/shard_map/ppermute | solution.py:389
  7.5 0.7 %copy-done = s32[16]{0:T(128)S(1)} copy-done((s32[16]{0:T(128)S(1)}, s32[16]{0:T(128)}, u32[]{:S(2)}) %copy-start) | copy-done | bytes 88
  8.2 7.5 %gen_attention.1 = (bf16[16,64,128]{2,1,0:T(8,128)(2,1)S(1)}, f32[16,64,128]{2,1,0:T(8,128)S(1)}, f32[16,64,128]{2,1,0:T(8,128)S(1)}) custom-call(s32[16]{0:T(128)S(1)} %copy-done, bf16[4,16,2048]{2,1,0:T(8,128)(2,1)} %q_ref.1, bf16[4,16,512]{2,1,0:T(8,128)(2,1)} %new_ref.1, bf16[16,512,512]{2,1,0:T(8,128)(2,1)} %kv_ref.1), custom_call_target="tpu_custom_call" | custom-call | flops 268435456 | bytes 8388608 | tf_op jit(solution)/shard_map/gen_attention/pallas_call | solution.py:145
  15.7 3.6 %collective-permute-start.3 = (bf16[520,128]{1,0:T(8,128)(2,1)S(1)}, bf16[520,128]{1,0:T(8,128)(2,1)S(1)}, u32[]{:S(2)}, u32[]{:S(2)}) collective-permute-start(bf16[520,128]{1,0:T(8,128)(2,1)S(1)} %slice.9), channel_id=1, source_target_pairs={{0,4},{4,0},{8,12},{12,8},{1,5},{5,1},{9,13},{13,9},{2,6},{6,2},{1... | collective-permute-start | bytes 399368 | tf_op jit(solution)/shard_map/ppermute | solution.py:389
  19.3 1.4 %shard_map.82.refs_0_ = bf16[32,2048]{1,0:T(8,128)(2,1)S(1)} custom-call(bf16[1032,128]{1,0:T(8,128)(2,1)S(1)} %get-tuple-element.24.refs_0_, bf16[1032,128]{1,0:T(8,128)(2,1)S(1)} %collective-permute-done.refs_1_, bf16[16,64,128]{2,1,0:T(8,128)(2,1)S(1)} %get-tuple-element.30.refs_2_.refs_3_, f32[16,64,128]{2,1,0:T(8,128)S(1)} %get-tuple-element.31.refs_3_.refs_4_, ...), custom_call_target="tpu_custom_call" | custom-call | flops 67108864 | bytes 524288 | tf_op jit(solution)/shard_map/pallas_call | solution.py:224
  20.7 2.5 %collective-permute-start.7 = (bf16[32,2048]{1,0:T(8,128)(2,1)S(1)}, bf16[32,2048]{1,0:T(8,128)(2,1)S(1)}, u32[]{:S(2)}, u32[]{:S(2)}) collective-permute-start(bf16[32,2048]{1,0:T(8,128)(2,1)S(1)} %shard_map.82.refs_0_), channel_id=1, source_target_pairs={{0,12},{4,8},{8,4},{12,0},{1,13},{5,9},{9,5},{13,1},{2,14},{6,10},... | collective-permute-start | bytes 393224 | tf_op jit(solution)/shard_map/ppermute | solution.py:389
  23.3 1.9 %collective-permute-start.9 = (bf16[32,2048]{1,0:T(8,128)(2,1)S(1)}, bf16[32,2048]{1,0:T(8,128)(2,1)S(1)}, u32[]{:S(2)}, u32[]{:S(2)}) collective-permute-start(bf16[32,2048]{1,0:T(8,128)(2,1)S(1)} %shard_map.82.refs_0_), channel_id=1, source_target_pairs={{0,4},{4,0},{8,12},{12,8},{1,5},{5,1},{9,13},{13,9},{2,6},{6,2},{1... | collective-permute-start | bytes 393224 | tf_op jit(solution)/shard_map/ppermute | solution.py:389
  25.2 3.9 %collective-permute-done.7.refs_2_ = bf16[32,2048]{1,0:T(8,128)(2,1)S(1)} collective-permute-done((bf16[32,2048]{1,0:T(8,128)(2,1)S(1)}, bf16[32,2048]{1,0:T(8,128)(2,1)S(1)}, u32[]{:S(2)}, u32[]{:S(2)}) %collective-permute-start.7) | collective-permute-done | bytes 131104 | tf_op jit(solution)/shard_map/ppermute | solution.py:389
  29.1 2.5 %collective-permute-start.8 = (bf16[32,2048]{1,0:T(8,128)(2,1)S(1)}, bf16[32,2048]{1,0:T(8,128)(2,1)S(1)}, u32[]{:S(2)}, u32[]{:S(2)}) collective-permute-start(bf16[32,2048]{1,0:T(8,128)(2,1)S(1)} %collective-permute-done.7.refs_2_), channel_id=1, source_target_pairs={{0,4},{4,0},{8,12},{12,8},{1,5},{5,1},{9,13},{13,9},{2,6},{6,2},{1... | collective-permute-start | bytes 393224 | tf_op jit(solution)/shard_map/ppermute | solution.py:389
  31.6 2.1 %collective-permute-done.2.refs_1_ = bf16[512,128]{1,0:T(8,128)(2,1)S(1)} collective-permute-done((bf16[512,128]{1,0:T(8,128)(2,1)S(1)}, bf16[512,128]{1,0:T(8,128)(2,1)S(1)}, u32[]{:S(2)}, u32[]{:S(2)}) %collective-permute-start.2) | collective-permute-done | bytes 131104 | tf_op jit(solution)/shard_map/ppermute | solution.py:389
  33.6 1.4 %shard_map.83.refs_1_ = bf16[32,2048]{1,0:T(8,128)(2,1)S(1)} custom-call(bf16[1032,128]{1,0:T(8,128)(2,1)S(1)} %collective-permute-done.1.refs_2_.refs_0_, bf16[512,128]{1,0:T(8,128)(2,1)S(1)} %collective-permute-done.2.refs_1_, bf16[520,128]{1,0:T(8,128)(2,1)S(1)} %collective-permute-done.3.refs_3_.refs_2_, ...), custom_call_target="tpu_custom_call" | custom-call | flops 67108864 | bytes 524288 | tf_op jit(solution)/shard_map/pallas_call | solution.py:224
  35.1 3.0 %collective-permute-start.5 = (bf16[32,2048]{1,0:T(8,128)(2,1)S(1)}, bf16[32,2048]{1,0:T(8,128)(2,1)S(1)}, u32[]{:S(2)}, u32[]{:S(2)}) collective-permute-start(bf16[32,2048]{1,0:T(8,128)(2,1)S(1)} %shard_map.83.refs_1_), channel_id=1, source_target_pairs={{0,4},{4,0},{8,12},{12,8},{1,5},{5,1},{9,13},{13,9},{2,6},{6,2},{1... | collective-permute-start | bytes 393224 | tf_op jit(solution)/shard_map/ppermute | solution.py:389
  38.2 1.3 %collective-permute-start.4 = (bf16[32,2048]{1,0:T(8,128)(2,1)S(1)}, bf16[32,2048]{1,0:T(8,128)(2,1)S(1)}, u32[]{:S(2)}, u32[]{:S(2)}) collective-permute-start(bf16[32,2048]{1,0:T(8,128)(2,1)S(1)} %shard_map.83.refs_1_), channel_id=1, source_target_pairs={{0,12},{4,8},{8,4},{12,0},{1,13},{5,9},{9,5},{13,1},{2,14},{6,10},... | collective-permute-start | bytes 393224 | tf_op jit(solution)/shard_map/ppermute | solution.py:389
  39.5 2.2 %hold.1.refs_4_.refs_5_ = bf16[2048,1024]{1,0:T(8,128)(2,1)S(1)} custom-call(bf16[2048,1024]{1,0:T(8,128)(2,1)} %w_ref.1), custom_call_target="tpu_custom_call" | custom-call | tf_op jit(solution)/shard_map/hold/pallas_call | solution.py:296
  41.7 0.7 %project_first.1.refs_4_ = f32[128,1024]{1,0:T(8,128)S(1)} custom-call(bf16[32,2048]{1,0:T(8,128)(2,1)S(1)} %shard_map.82.refs_0_, bf16[32,2048]{1,0:T(8,128)(2,1)S(1)} %shard_map.83.refs_1_, bf16[32,2048]{1,0:T(8,128)(2,1)S(1)} %collective-permute-done.7.refs_2_, bf16[32,2048]{1,0:T(8,128)(2,1)S(1)} %collective-permute-done.9.refs_3_, ...), custom_call_target="tpu_custom_call" | custom-call | flops 536870912 | bytes 4194304 | tf_op jit(solution)/shard_map/project_first/pallas_call | solution.py:325
  42.5 4.1 %collective-permute-done.6.refs_2_ = bf16[32,2048]{1,0:T(8,128)(2,1)S(1)} collective-permute-done((bf16[32,2048]{1,0:T(8,128)(2,1)S(1)}, bf16[32,2048]{1,0:T(8,128)(2,1)S(1)}, u32[]{:S(2)}, u32[]{:S(2)}) %collective-permute-start.6) | collective-permute-done | bytes 131104 | tf_op jit(solution)/shard_map/ppermute | solution.py:389
  46.6 0.8 %project_last.1 = (f32[2,64,1024]{2,1,0:T(8,128)S(1)}, f32[2,64,1024]{2,1,0:T(8,128)S(1)}) custom-call(bf16[32,2048]{1,0:T(8,128)(2,1)S(1)} %collective-permute-done.4.refs_0_, bf16[32,2048]{1,0:T(8,128)(2,1)S(1)} %collective-permute-done.5.refs_1_, bf16[32,2048]{1,0:T(8,128)(2,1)S(1)} %collective-permute-done.6.refs_2_, ...), custom_call_target="tpu_custom_call" | custom-call | flops 536870912 | bytes 4194304 | tf_op jit(solution)/shard_map/project_last/pallas_call | solution.py:369
  47.5 1.9 %collective-permute-done.10 = f32[2,64,1024]{2,1,0:T(8,128)S(1)} collective-permute-done((f32[2,64,1024]{2,1,0:T(8,128)S(1)}, f32[2,64,1024]{2,1,0:T(8,128)S(1)}, u32[]{:S(2)}, u32[]{:S(2)}) %collective-permute-start.10) | collective-permute-done | bytes 524320 | tf_op jit(solution)/shard_map/ppermute | solution.py:423
  49.5 3.1 %collective-permute-start.12 = (bf16[64,1024]{1,0:T(8,128)(2,1)S(1)}, bf16[64,1024]{1,0:T(8,128)(2,1)S(1)}, u32[]{:S(2)}, u32[]{:S(2)}) collective-permute-start(bf16[64,1024]{1,0:T(8,128)(2,1)S(1)} %get-tuple-element.43), channel_id=1, source_target_pairs={{0,8},{1,0},{2,12},{3,4},{4,9},{5,1},{6,13},{7,5},{8,10},{9,2},{10... | collective-permute-start | bytes 393224 | tf_op jit(solution)/shard_map/ppermute | solution.py:431
  52.6 4.0 %collective-permute-start.11 = (bf16[64,1024]{1,0:T(8,128)(2,1)S(1)}, bf16[64,1024]{1,0:T(8,128)(2,1)S(1)}, u32[]{:S(2)}, u32[]{:S(2)}) collective-permute-start(bf16[64,1024]{1,0:T(8,128)(2,1)S(1)} %get-tuple-element.44), channel_id=1, source_target_pairs={{0,12},{1,4},{2,8},{3,0},{4,13},{5,5},{6,9},{7,1},{8,14},{9,6},{10... | collective-permute-start | bytes 393224 | tf_op jit(solution)/shard_map/ppermute | solution.py:431
  56.7 0.1 row_order.1.order_ref
  56.8 2.6 %collective-permute-done.11.a_ref = bf16[64,1024]{1,0:T(8,128)(2,1)S(1)} collective-permute-done((bf16[64,1024]{1,0:T(8,128)(2,1)S(1)}, bf16[64,1024]{1,0:T(8,128)(2,1)S(1)}, u32[]{:S(2)}, u32[]{:S(2)}) %collective-permute-start.11) | collective-permute-done | bytes 131104 | tf_op jit(solution)/shard_map/ppermute | solution.py:431
  59.4 0.8 %finish.1 = bf16[64,1024]{1,0:T(8,128)(2,1)} custom-call(bf16[64,64]{1,0:T(8,128)(2,1)S(1)} %row_order.1.order_ref, bf16[64,1024]{1,0:T(8,128)(2,1)S(1)} %collective-permute-done.11.a_ref, bf16[64,1024]{1,0:T(8,128)(2,1)S(1)} %collective-permute-done.12.b_ref), custom_call_target="tpu_custom_call" | custom-call | tf_op jit(solution)/shard_map/finish/pallas_call | solution.py:274
  (16 shorter events, 0.3 us)
Async XLA Ops:
  2.4 13.3 %collective-permute-start = (bf16[1032,128]{1,0:T(8,128)(2,1)S(1)}, bf16[1032,128]{1,0:T(8,128)(2,1)S(1)}, u32[]{:S(2)}, u32[]{:S(2)}) collective-permute-start(bf16[1032,128]{1,0:T(8,128)(2,1)S(1)} %get-tuple-element.24.refs_0_), channel_id=1, source_target_pairs={{0,12},{4,8},{8,4},{12,0},{1,13},{5,9},{9,5},{13,1},{2,14},{6,10},... | collective-permute-start | bytes 792584 | tf_op jit(solution)/shard_map/ppermute | solution.py:389
  7.5 26.1 %collective-permute-start.1 = (bf16[1032,128]{1,0:T(8,128)(2,1)S(1)}, bf16[1032,128]{1,0:T(8,128)(2,1)S(1)}, u32[]{:S(2)}, u32[]{:S(2)}) collective-permute-start(bf16[1032,128]{1,0:T(8,128)(2,1)S(1)} %get-tuple-element.24.refs_0_), channel_id=1, source_target_pairs={{0,4},{4,0},{8,12},{12,8},{1,5},{5,1},{9,13},{13,9},{2,6},{6,2},{1... | collective-permute-start | bytes 792584 | tf_op jit(solution)/shard_map/ppermute | solution.py:389
  7.5 0.7 %copy-start = (s32[16]{0:T(128)S(1)}, s32[16]{0:T(128)}, u32[]{:S(2)}) copy-start(s32[16]{0:T(128)} %len_ref.1) | copy-start | bytes 196
  15.7 17.9 %collective-permute-start.3 = (bf16[520,128]{1,0:T(8,128)(2,1)S(1)}, bf16[520,128]{1,0:T(8,128)(2,1)S(1)}, u32[]{:S(2)}, u32[]{:S(2)}) collective-permute-start(bf16[520,128]{1,0:T(8,128)(2,1)S(1)} %slice.9), channel_id=1, source_target_pairs={{0,4},{4,0},{8,12},{12,8},{1,5},{5,1},{9,13},{13,9},{2,6},{6,2},{1... | collective-permute-start | bytes 399368 | tf_op jit(solution)/shard_map/ppermute | solution.py:389
  20.7 8.3 %collective-permute-start.7 = (bf16[32,2048]{1,0:T(8,128)(2,1)S(1)}, bf16[32,2048]{1,0:T(8,128)(2,1)S(1)}, u32[]{:S(2)}, u32[]{:S(2)}) collective-permute-start(bf16[32,2048]{1,0:T(8,128)(2,1)S(1)} %shard_map.82.refs_0_), channel_id=1, source_target_pairs={{0,12},{4,8},{8,4},{12,0},{1,13},{5,9},{9,5},{13,1},{2,14},{6,10},... | collective-permute-start | bytes 393224 | tf_op jit(solution)/shard_map/ppermute | solution.py:389
  23.3 10.4 %collective-permute-start.2 = (bf16[512,128]{1,0:T(8,128)(2,1)S(1)}, bf16[512,128]{1,0:T(8,128)(2,1)S(1)}, u32[]{:S(2)}, u32[]{:S(2)}) collective-permute-start(bf16[512,128]{1,0:T(8,128)(2,1)S(1)} %get-tuple-element.29), channel_id=1, source_target_pairs={{0,8},{4,12},{8,0},{12,4},{1,9},{5,13},{9,1},{13,5},{2,10},{6,14},... | collective-permute-start | bytes 393224 | tf_op jit(solution)/shard_map/ppermute | solution.py:389
  23.3 18.4 %collective-permute-start.9 = (bf16[32,2048]{1,0:T(8,128)(2,1)S(1)}, bf16[32,2048]{1,0:T(8,128)(2,1)S(1)}, u32[]{:S(2)}, u32[]{:S(2)}) collective-permute-start(bf16[32,2048]{1,0:T(8,128)(2,1)S(1)} %shard_map.82.refs_0_), channel_id=1, source_target_pairs={{0,4},{4,0},{8,12},{12,8},{1,5},{5,1},{9,13},{13,9},{2,6},{6,2},{1... | collective-permute-start | bytes 393224 | tf_op jit(solution)/shard_map/ppermute | solution.py:389
  29.1 13.4 %collective-permute-start.8 = (bf16[32,2048]{1,0:T(8,128)(2,1)S(1)}, bf16[32,2048]{1,0:T(8,128)(2,1)S(1)}, u32[]{:S(2)}, u32[]{:S(2)}) collective-permute-start(bf16[32,2048]{1,0:T(8,128)(2,1)S(1)} %collective-permute-done.7.refs_2_), channel_id=1, source_target_pairs={{0,4},{4,0},{8,12},{12,8},{1,5},{5,1},{9,13},{13,9},{2,6},{6,2},{1... | collective-permute-start | bytes 393224 | tf_op jit(solution)/shard_map/ppermute | solution.py:389
  35.0 11.6 %collective-permute-start.6 = (bf16[32,2048]{1,0:T(8,128)(2,1)S(1)}, bf16[32,2048]{1,0:T(8,128)(2,1)S(1)}, u32[]{:S(2)}, u32[]{:S(2)}) collective-permute-start(bf16[32,2048]{1,0:T(8,128)(2,1)S(1)} %shard_map.83.refs_1_), channel_id=1, source_target_pairs={{0,8},{4,12},{8,0},{12,4},{1,9},{5,13},{9,1},{13,5},{2,10},{6,14},... | collective-permute-start | bytes 393224 | tf_op jit(solution)/shard_map/ppermute | solution.py:389
  35.1 11.5 %collective-permute-start.5 = (bf16[32,2048]{1,0:T(8,128)(2,1)S(1)}, bf16[32,2048]{1,0:T(8,128)(2,1)S(1)}, u32[]{:S(2)}, u32[]{:S(2)}) collective-permute-start(bf16[32,2048]{1,0:T(8,128)(2,1)S(1)} %shard_map.83.refs_1_), channel_id=1, source_target_pairs={{0,4},{4,0},{8,12},{12,8},{1,5},{5,1},{9,13},{13,9},{2,6},{6,2},{1... | collective-permute-start | bytes 393224 | tf_op jit(solution)/shard_map/ppermute | solution.py:389
  38.2 8.5 %collective-permute-start.4 = (bf16[32,2048]{1,0:T(8,128)(2,1)S(1)}, bf16[32,2048]{1,0:T(8,128)(2,1)S(1)}, u32[]{:S(2)}, u32[]{:S(2)}) collective-permute-start(bf16[32,2048]{1,0:T(8,128)(2,1)S(1)} %shard_map.83.refs_1_), channel_id=1, source_target_pairs={{0,12},{4,8},{8,4},{12,0},{1,13},{5,9},{9,5},{13,1},{2,14},{6,10},... | collective-permute-start | bytes 393224 | tf_op jit(solution)/shard_map/ppermute | solution.py:389
  47.4 2.0 %collective-permute-start.10 = (f32[2,64,1024]{2,1,0:T(8,128)S(1)}, f32[2,64,1024]{2,1,0:T(8,128)S(1)}, u32[]{:S(2)}, u32[]{:S(2)}) collective-permute-start(f32[2,64,1024]{2,1,0:T(8,128)S(1)} %get-tuple-element.42), channel_id=1, source_target_pairs={{0,1},{1,0},{2,3},{3,2},{4,5},{5,4},{6,7},{7,6},{8,9},{9,8},{10,11... | collective-permute-start | bytes 1572872 | tf_op jit(solution)/shard_map/ppermute | solution.py:423
  49.5 7.3 %collective-permute-start.12 = (bf16[64,1024]{1,0:T(8,128)(2,1)S(1)}, bf16[64,1024]{1,0:T(8,128)(2,1)S(1)}, u32[]{:S(2)}, u32[]{:S(2)}) collective-permute-start(bf16[64,1024]{1,0:T(8,128)(2,1)S(1)} %get-tuple-element.43), channel_id=1, source_target_pairs={{0,8},{1,0},{2,12},{3,4},{4,9},{5,1},{6,13},{7,5},{8,10},{9,2},{10... | collective-permute-start | bytes 393224 | tf_op jit(solution)/shard_map/ppermute | solution.py:431
  52.6 6.7 %collective-permute-start.11 = (bf16[64,1024]{1,0:T(8,128)(2,1)S(1)}, bf16[64,1024]{1,0:T(8,128)(2,1)S(1)}, u32[]{:S(2)}, u32[]{:S(2)}) collective-permute-start(bf16[64,1024]{1,0:T(8,128)(2,1)S(1)} %get-tuple-element.44), channel_id=1, source_target_pairs={{0,12},{1,4},{2,8},{3,0},{4,13},{5,5},{6,9},{7,1},{8,14},{9,6},{10... | collective-permute-start | bytes 393224 | tf_op jit(solution)/shard_map/ppermute | solution.py:431

commit v4 on v3

--- a/solution.py
+++ b/solution.py
@@ -357,7 +357,7 @@
     half = blocks // 2
     for k in range(half):
         keep_ref[k] = both[k]
-        send_ref[k] = both[half + k]
+        send_ref[k] = both[half + k].astype(send_ref.dtype)
 
 
 def project_last(pieces, homes, first, first_homes, weight, block):
@@ -368,7 +368,7 @@
     shape = jax.ShapeDtypeStruct((blocks // 2, block, cols), jnp.float32)
     return pl.pallas_call(
         functools.partial(project_last_kernel, blocks, first_homes, homes),
-        out_shape=(shape, shape),
+        out_shape=(shape, jax.ShapeDtypeStruct(shape.shape, jnp.bfloat16)),
         in_specs=[vmem] * (len(pieces) + 2),
         out_specs=(vmem, vmem),
         scratch_shapes=[
@@ -399,7 +399,7 @@
     far = exchange(payload, size, 3)
     near = exchange(payload, size, 1)
     direct_half = exchange(part, size, 2)
-    grouped, acc, ml = gen_attention(queries, new_kv, gen_kv, gen_len, heads, 4)
+    grouped, acc, ml = gen_attention(queries, new_kv, gen_kv, gen_len, heads, 8)
     far, grouped, acc, ml = lax.optimization_barrier((far, grouped, acc, ml))
     diag = exchange(far[part.shape[0] :], size, 1)
     most = add_slots(grouped, acc, ml, [[payload], [far]], size, steps, heads, keys)

time: 61 us -> 60.6 us (level)
  Pallas kernels: 16.1 us -> 15 us
  starting transfers between devices: 27.4 us -> 28.3 us
    pallas_call x1, Pallas kernels: 7.5 us -> 6.48 us  [gen_attention(): pl.pallas_call(functools.partial(gen_kernel, steps, heads, group), out_sh...]
    ppermute x10, starting transfers between devices: 20.2 us -> 21.1 us  [exchange(): return lax.ppermute(x, 'sample', [(i, i ^ flip) for i in range(size)])]
  transfers between devices with their start and end apart: 13 -> 13, of which waited for: 5 -> 6; matrix products, arithmetic and copies ran while one was open for 0% -> 0% of each run, Pallas kernels for 22% -> 21%
where the time goes in v4:
time: 60.6 us; the launch traced here: 59.8 us
  starting transfers between devices  28.3 us (47%)
  Pallas kernels  15 us (25%)
  waiting for transfers between devices  14.4 us (24%)
  between operations  1.41 us (2%)
  local copies, waits for them, and re-layouts  0.68 us (1%)
    ppermute x10, starting transfers between devices, exchange(): return lax.ppermute(x, 'sample', [(i, i ^ flip) for i in range(size)])  21.1 us
    ppermute x10, waiting for transfers between devices, exchange(): return lax.ppermute(x, 'sample', [(i, i ^ flip) for i in range(size)])  10.3 us
    ppermute x2, starting transfers between devices, direct(): piece = lax.ppermute(halves[i], ('sample', 'tensor'), perm)  7.17 us
    pallas_call x1, Pallas kernels, gen_attention(): pl.pallas_call(functools.partial(gen_kernel, steps, heads, group), out_sh...  6.48 us
    pallas_call x2, Pallas kernels, add_slots(): pl.pallas_call(functools.partial(add_slots_kernel, slots, steps, group, h...  2.8 us
    ppermute x2, waiting for transfers between devices, direct(): piece = lax.ppermute(halves[i], ('sample', 'tensor'), perm)  2.56 us
    pallas_call x1, Pallas kernels, hold(): pl.pallas_call(hold_kernel, out_shape=jax.ShapeDtypeStruct(weight.shape,...  2.2 us
    ppermute x1, waiting for transfers between devices, direct(): got = lax.ppermute(send, 'tensor', [(0, 1), (1, 0), (2, 3), (3, 2)])  1.52 us
  transfers between devices with their start and end apart: 13, of which 6 were waited for; matrix products, arithmetic and copies ran while one was open for 0% of the time, Pallas kernels for 21%

profile of v4, /device:TPU:0, one launch (start us, length us, event | category | flops | bytes accessed | tf_op | source)
XLA Modules:
  0.0 59.8 jit_solution(2082408494014436399)
XLA Ops:
  1.3 1.1 %make_payload.1 = (bf16[1032,128]{1,0:T(8,128)(2,1)S(1)}, bf16[512,128]{1,0:T(8,128)(2,1)S(1)}) custom-call(s32[1]{0:T(128)S(6)} %copy.9.prompt_ref, s32[1]{0:T(128)S(6)} %copy.10.blocks_ref, bf16[1,256,512]{2,1,0:T(8,128)(2,1)} %pre_ref.1), custom_call_target="tpu_custom_call" | custom-call | tf_op jit(solution)/shard_map/make_payload/pallas_call | solution.py:54
  2.4 5.1 %collective-permute-start = (bf16[1032,128]{1,0:T(8,128)(2,1)S(1)}, bf16[1032,128]{1,0:T(8,128)(2,1)S(1)}, u32[]{:S(2)}, u32[]{:S(2)}) collective-permute-start(bf16[1032,128]{1,0:T(8,128)(2,1)S(1)} %get-tuple-element.24.refs_0_), channel_id=1, source_target_pairs={{0,12},{4,8},{8,4},{12,0},{1,13},{5,9},{9,5},{13,1},{2,14},{6,10},... | collective-permute-start | bytes 792584 | tf_op jit(solution)/shard_map/ppermute | solution.py:389
  7.5 0.7 %copy-done = s32[16]{0:T(128)S(1)} copy-done((s32[16]{0:T(128)S(1)}, s32[16]{0:T(128)}, u32[]{:S(2)}) %copy-start) | copy-done | bytes 88
  8.2 6.5 %gen_attention.1 = (bf16[16,64,128]{2,1,0:T(8,128)(2,1)S(1)}, f32[16,64,128]{2,1,0:T(8,128)S(1)}, f32[16,64,128]{2,1,0:T(8,128)S(1)}) custom-call(s32[16]{0:T(128)S(1)} %copy-done, bf16[4,16,2048]{2,1,0:T(8,128)(2,1)} %q_ref.1, bf16[4,16,512]{2,1,0:T(8,128)(2,1)} %new_ref.1, bf16[16,512,512]{2,1,0:T(8,128)(2,1)} %kv_ref.1), custom_call_target="tpu_custom_call" | custom-call | flops 268435456 | bytes 8388608 | tf_op jit(solution)/shard_map/gen_attention/pallas_call | solution.py:145
  14.7 0.1 collective-permute-done.refs_1_
  14.8 4.5 %collective-permute-start.3 = (bf16[520,128]{1,0:T(8,128)(2,1)S(1)}, bf16[520,128]{1,0:T(8,128)(2,1)S(1)}, u32[]{:S(2)}, u32[]{:S(2)}) collective-permute-start(bf16[520,128]{1,0:T(8,128)(2,1)S(1)} %slice.9), channel_id=1, source_target_pairs={{0,4},{4,0},{8,12},{12,8},{1,5},{5,1},{9,13},{13,9},{2,6},{6,2},{1... | collective-permute-start | bytes 399368 | tf_op jit(solution)/shard_map/ppermute | solution.py:389
  19.3 1.4 %shard_map.82.refs_0_ = bf16[32,2048]{1,0:T(8,128)(2,1)S(1)} custom-call(bf16[1032,128]{1,0:T(8,128)(2,1)S(1)} %get-tuple-element.24.refs_0_, bf16[1032,128]{1,0:T(8,128)(2,1)S(1)} %collective-permute-done.refs_1_, bf16[16,64,128]{2,1,0:T(8,128)(2,1)S(1)} %get-tuple-element.30.refs_2_.refs_3_, f32[16,64,128]{2,1,0:T(8,128)S(1)} %get-tuple-element.31.refs_3_.refs_4_, ...), custom_call_target="tpu_custom_call" | custom-call | flops 67108864 | bytes 524288 | tf_op jit(solution)/shard_map/pallas_call | solution.py:224
  20.7 2.5 %collective-permute-start.7 = (bf16[32,2048]{1,0:T(8,128)(2,1)S(1)}, bf16[32,2048]{1,0:T(8,128)(2,1)S(1)}, u32[]{:S(2)}, u32[]{:S(2)}) collective-permute-start(bf16[32,2048]{1,0:T(8,128)(2,1)S(1)} %shard_map.82.refs_0_), channel_id=1, source_target_pairs={{0,12},{4,8},{8,4},{12,0},{1,13},{5,9},{9,5},{13,1},{2,14},{6,10},... | collective-permute-start | bytes 393224 | tf_op jit(solution)/shard_map/ppermute | solution.py:389
  23.3 1.9 %collective-permute-start.9 = (bf16[32,2048]{1,0:T(8,128)(2,1)S(1)}, bf16[32,2048]{1,0:T(8,128)(2,1)S(1)}, u32[]{:S(2)}, u32[]{:S(2)}) collective-permute-start(bf16[32,2048]{1,0:T(8,128)(2,1)S(1)} %shard_map.82.refs_0_), channel_id=1, source_target_pairs={{0,4},{4,0},{8,12},{12,8},{1,5},{5,1},{9,13},{13,9},{2,6},{6,2},{1... | collective-permute-start | bytes 393224 | tf_op jit(solution)/shard_map/ppermute | solution.py:389
  25.2 3.9 %collective-permute-done.7.refs_2_ = bf16[32,2048]{1,0:T(8,128)(2,1)S(1)} collective-permute-done((bf16[32,2048]{1,0:T(8,128)(2,1)S(1)}, bf16[32,2048]{1,0:T(8,128)(2,1)S(1)}, u32[]{:S(2)}, u32[]{:S(2)}) %collective-permute-start.7) | collective-permute-done | bytes 131104 | tf_op jit(solution)/shard_map/ppermute | solution.py:389
  29.1 2.5 %collective-permute-start.8 = (bf16[32,2048]{1,0:T(8,128)(2,1)S(1)}, bf16[32,2048]{1,0:T(8,128)(2,1)S(1)}, u32[]{:S(2)}, u32[]{:S(2)}) collective-permute-start(bf16[32,2048]{1,0:T(8,128)(2,1)S(1)} %collective-permute-done.7.refs_2_), channel_id=1, source_target_pairs={{0,4},{4,0},{8,12},{12,8},{1,5},{5,1},{9,13},{13,9},{2,6},{6,2},{1... | collective-permute-start | bytes 393224 | tf_op jit(solution)/shard_map/ppermute | solution.py:389
  31.6 2.1 %collective-permute-done.2.refs_1_ = bf16[512,128]{1,0:T(8,128)(2,1)S(1)} collective-permute-done((bf16[512,128]{1,0:T(8,128)(2,1)S(1)}, bf16[512,128]{1,0:T(8,128)(2,1)S(1)}, u32[]{:S(2)}, u32[]{:S(2)}) %collective-permute-start.2) | collective-permute-done | bytes 131104 | tf_op jit(solution)/shard_map/ppermute | solution.py:389
  33.6 1.4 %shard_map.83.refs_1_ = bf16[32,2048]{1,0:T(8,128)(2,1)S(1)} custom-call(bf16[1032,128]{1,0:T(8,128)(2,1)S(1)} %collective-permute-done.1.refs_2_.refs_0_, bf16[512,128]{1,0:T(8,128)(2,1)S(1)} %collective-permute-done.2.refs_1_, bf16[520,128]{1,0:T(8,128)(2,1)S(1)} %collective-permute-done.3.refs_3_.refs_2_, ...), custom_call_target="tpu_custom_call" | custom-call | flops 67108864 | bytes 524288 | tf_op jit(solution)/shard_map/pallas_call | solution.py:224
  35.1 3.0 %collective-permute-start.5 = (bf16[32,2048]{1,0:T(8,128)(2,1)S(1)}, bf16[32,2048]{1,0:T(8,128)(2,1)S(1)}, u32[]{:S(2)}, u32[]{:S(2)}) collective-permute-start(bf16[32,2048]{1,0:T(8,128)(2,1)S(1)} %shard_map.83.refs_1_), channel_id=1, source_target_pairs={{0,4},{4,0},{8,12},{12,8},{1,5},{5,1},{9,13},{13,9},{2,6},{6,2},{1... | collective-permute-start | bytes 393224 | tf_op jit(solution)/shard_map/ppermute | solution.py:389
  38.2 1.3 %collective-permute-start.4 = (bf16[32,2048]{1,0:T(8,128)(2,1)S(1)}, bf16[32,2048]{1,0:T(8,128)(2,1)S(1)}, u32[]{:S(2)}, u32[]{:S(2)}) collective-permute-start(bf16[32,2048]{1,0:T(8,128)(2,1)S(1)} %shard_map.83.refs_1_), channel_id=1, source_target_pairs={{0,12},{4,8},{8,4},{12,0},{1,13},{5,9},{9,5},{13,1},{2,14},{6,10},... | collective-permute-start | bytes 393224 | tf_op jit(solution)/shard_map/ppermute | solution.py:389
  39.5 2.2 %hold.1.refs_4_.refs_5_ = bf16[2048,1024]{1,0:T(8,128)(2,1)S(1)} custom-call(bf16[2048,1024]{1,0:T(8,128)(2,1)} %w_ref.1), custom_call_target="tpu_custom_call" | custom-call | tf_op jit(solution)/shard_map/hold/pallas_call | solution.py:296
  41.7 0.7 %project_first.1.refs_4_ = f32[128,1024]{1,0:T(8,128)S(1)} custom-call(bf16[32,2048]{1,0:T(8,128)(2,1)S(1)} %shard_map.82.refs_0_, bf16[32,2048]{1,0:T(8,128)(2,1)S(1)} %shard_map.83.refs_1_, bf16[32,2048]{1,0:T(8,128)(2,1)S(1)} %collective-permute-done.7.refs_2_, bf16[32,2048]{1,0:T(8,128)(2,1)S(1)} %collective-permute-done.9.refs_3_, ...), custom_call_target="tpu_custom_call" | custom-call | flops 536870912 | bytes 4194304 | tf_op jit(solution)/shard_map/project_first/pallas_call | solution.py:325
  42.5 4.1 %collective-permute-done.6.refs_2_ = bf16[32,2048]{1,0:T(8,128)(2,1)S(1)} collective-permute-done((bf16[32,2048]{1,0:T(8,128)(2,1)S(1)}, bf16[32,2048]{1,0:T(8,128)(2,1)S(1)}, u32[]{:S(2)}, u32[]{:S(2)}) %collective-permute-start.6) | collective-permute-done | bytes 131104 | tf_op jit(solution)/shard_map/ppermute | solution.py:389
  46.6 0.8 %project_last.1 = (f32[2,64,1024]{2,1,0:T(8,128)S(1)}, bf16[2,64,1024]{2,1,0:T(8,128)(2,1)S(1)}) custom-call(bf16[32,2048]{1,0:T(8,128)(2,1)S(1)} %collective-permute-done.4.refs_0_, bf16[32,2048]{1,0:T(8,128)(2,1)S(1)} %collective-permute-done.5.refs_1_, bf16[32,2048]{1,0:T(8,128)(2,1)S(1)} %collective-permute-done.6.refs_2_, ...), custom_call_target="tpu_custom_call" | custom-call | flops 536870912 | bytes 4194304 | tf_op jit(solution)/shard_map/project_last/pallas_call | solution.py:369
  47.5 1.5 %collective-permute-done.10 = bf16[2,64,1024]{2,1,0:T(8,128)(2,1)S(1)} collective-permute-done((bf16[2,64,1024]{2,1,0:T(8,128)(2,1)S(1)}, bf16[2,64,1024]{2,1,0:T(8,128)(2,1)S(1)}, u32[]{:S(2)}, u32[]{:S(2)}) %collective-permute-start.10) | collective-permute-done | bytes 262176 | tf_op jit(solution)/shard_map/ppermute | solution.py:423
  49.1 3.1 %collective-permute-start.12 = (bf16[64,1024]{1,0:T(8,128)(2,1)S(1)}, bf16[64,1024]{1,0:T(8,128)(2,1)S(1)}, u32[]{:S(2)}, u32[]{:S(2)}) collective-permute-start(bf16[64,1024]{1,0:T(8,128)(2,1)S(1)} %get-tuple-element.43), channel_id=1, source_target_pairs={{0,8},{1,0},{2,12},{3,4},{4,9},{5,1},{6,13},{7,5},{8,10},{9,2},{10... | collective-permute-start | bytes 393224 | tf_op jit(solution)/shard_map/ppermute | solution.py:431
  52.3 4.0 %collective-permute-start.11 = (bf16[64,1024]{1,0:T(8,128)(2,1)S(1)}, bf16[64,1024]{1,0:T(8,128)(2,1)S(1)}, u32[]{:S(2)}, u32[]{:S(2)}) collective-permute-start(bf16[64,1024]{1,0:T(8,128)(2,1)S(1)} %get-tuple-element.44), channel_id=1, source_target_pairs={{0,12},{1,4},{2,8},{3,0},{4,13},{5,5},{6,9},{7,1},{8,14},{9,6},{10... | collective-permute-start | bytes 393224 | tf_op jit(solution)/shard_map/ppermute | solution.py:431
  56.4 2.6 %collective-permute-done.11.a_ref = bf16[64,1024]{1,0:T(8,128)(2,1)S(1)} collective-permute-done((bf16[64,1024]{1,0:T(8,128)(2,1)S(1)}, bf16[64,1024]{1,0:T(8,128)(2,1)S(1)}, u32[]{:S(2)}, u32[]{:S(2)}) %collective-permute-start.11) | collective-permute-done | bytes 131104 | tf_op jit(solution)/shard_map/ppermute | solution.py:431
  59.0 0.8 %finish.1 = bf16[64,1024]{1,0:T(8,128)(2,1)} custom-call(bf16[64,64]{1,0:T(8,128)(2,1)S(1)} %row_order.1.order_ref, bf16[64,1024]{1,0:T(8,128)(2,1)S(1)} %collective-permute-done.11.a_ref, bf16[64,1024]{1,0:T(8,128)(2,1)S(1)} %collective-permute-done.12.b_ref), custom_call_target="tpu_custom_call" | custom-call | tf_op jit(solution)/shard_map/finish/pallas_call | solution.py:274
  (16 shorter events, 0.4 us)
Async XLA Ops:
  2.4 12.4 %collective-permute-start = (bf16[1032,128]{1,0:T(8,128)(2,1)S(1)}, bf16[1032,128]{1,0:T(8,128)(2,1)S(1)}, u32[]{:S(2)}, u32[]{:S(2)}) collective-permute-start(bf16[1032,128]{1,0:T(8,128)(2,1)S(1)} %get-tuple-element.24.refs_0_), channel_id=1, source_target_pairs={{0,12},{4,8},{8,4},{12,0},{1,13},{5,9},{9,5},{13,1},{2,14},{6,10},... | collective-permute-start | bytes 792584 | tf_op jit(solution)/shard_map/ppermute | solution.py:389
  7.5 26.1 %collective-permute-start.1 = (bf16[1032,128]{1,0:T(8,128)(2,1)S(1)}, bf16[1032,128]{1,0:T(8,128)(2,1)S(1)}, u32[]{:S(2)}, u32[]{:S(2)}) collective-permute-start(bf16[1032,128]{1,0:T(8,128)(2,1)S(1)} %get-tuple-element.24.refs_0_), channel_id=1, source_target_pairs={{0,4},{4,0},{8,12},{12,8},{1,5},{5,1},{9,13},{13,9},{2,6},{6,2},{1... | collective-permute-start | bytes 792584 | tf_op jit(solution)/shard_map/ppermute | solution.py:389
  7.5 0.7 %copy-start = (s32[16]{0:T(128)S(1)}, s32[16]{0:T(128)}, u32[]{:S(2)}) copy-start(s32[16]{0:T(128)} %len_ref.1) | copy-start | bytes 196
  14.8 18.8 %collective-permute-start.3 = (bf16[520,128]{1,0:T(8,128)(2,1)S(1)}, bf16[520,128]{1,0:T(8,128)(2,1)S(1)}, u32[]{:S(2)}, u32[]{:S(2)}) collective-permute-start(bf16[520,128]{1,0:T(8,128)(2,1)S(1)} %slice.9), channel_id=1, source_target_pairs={{0,4},{4,0},{8,12},{12,8},{1,5},{5,1},{9,13},{13,9},{2,6},{6,2},{1... | collective-permute-start | bytes 399368 | tf_op jit(solution)/shard_map/ppermute | solution.py:389
  20.7 8.3 %collective-permute-start.7 = (bf16[32,2048]{1,0:T(8,128)(2,1)S(1)}, bf16[32,2048]{1,0:T(8,128)(2,1)S(1)}, u32[]{:S(2)}, u32[]{:S(2)}) collective-permute-start(bf16[32,2048]{1,0:T(8,128)(2,1)S(1)} %shard_map.82.refs_0_), channel_id=1, source_target_pairs={{0,12},{4,8},{8,4},{12,0},{1,13},{5,9},{9,5},{13,1},{2,14},{6,10},... | collective-permute-start | bytes 393224 | tf_op jit(solution)/shard_map/ppermute | solution.py:389
  23.3 10.4 %collective-permute-start.2 = (bf16[512,128]{1,0:T(8,128)(2,1)S(1)}, bf16[512,128]{1,0:T(8,128)(2,1)S(1)}, u32[]{:S(2)}, u32[]{:S(2)}) collective-permute-start(bf16[512,128]{1,0:T(8,128)(2,1)S(1)} %get-tuple-element.29), channel_id=1, source_target_pairs={{0,8},{4,12},{8,0},{12,4},{1,9},{5,13},{9,1},{13,5},{2,10},{6,14},... | collective-permute-start | bytes 393224 | tf_op jit(solution)/shard_map/ppermute | solution.py:389
  23.3 18.4 %collective-permute-start.9 = (bf16[32,2048]{1,0:T(8,128)(2,1)S(1)}, bf16[32,2048]{1,0:T(8,128)(2,1)S(1)}, u32[]{:S(2)}, u32[]{:S(2)}) collective-permute-start(bf16[32,2048]{1,0:T(8,128)(2,1)S(1)} %shard_map.82.refs_0_), channel_id=1, source_target_pairs={{0,4},{4,0},{8,12},{12,8},{1,5},{5,1},{9,13},{13,9},{2,6},{6,2},{1... | collective-permute-start | bytes 393224 | tf_op jit(solution)/shard_map/ppermute | solution.py:389
  29.1 13.4 %collective-permute-start.8 = (bf16[32,2048]{1,0:T(8,128)(2,1)S(1)}, bf16[32,2048]{1,0:T(8,128)(2,1)S(1)}, u32[]{:S(2)}, u32[]{:S(2)}) collective-permute-start(bf16[32,2048]{1,0:T(8,128)(2,1)S(1)} %collective-permute-done.7.refs_2_), channel_id=1, source_target_pairs={{0,4},{4,0},{8,12},{12,8},{1,5},{5,1},{9,13},{13,9},{2,6},{6,2},{1... | collective-permute-start | bytes 393224 | tf_op jit(solution)/shard_map/ppermute | solution.py:389
  35.0 11.6 %collective-permute-start.6 = (bf16[32,2048]{1,0:T(8,128)(2,1)S(1)}, bf16[32,2048]{1,0:T(8,128)(2,1)S(1)}, u32[]{:S(2)}, u32[]{:S(2)}) collective-permute-start(bf16[32,2048]{1,0:T(8,128)(2,1)S(1)} %shard_map.83.refs_1_), channel_id=1, source_target_pairs={{0,8},{4,12},{8,0},{12,4},{1,9},{5,13},{9,1},{13,5},{2,10},{6,14},... | collective-permute-start | bytes 393224 | tf_op jit(solution)/shard_map/ppermute | solution.py:389
  35.1 11.5 %collective-permute-start.5 = (bf16[32,2048]{1,0:T(8,128)(2,1)S(1)}, bf16[32,2048]{1,0:T(8,128)(2,1)S(1)}, u32[]{:S(2)}, u32[]{:S(2)}) collective-permute-start(bf16[32,2048]{1,0:T(8,128)(2,1)S(1)} %shard_map.83.refs_1_), channel_id=1, source_target_pairs={{0,4},{4,0},{8,12},{12,8},{1,5},{5,1},{9,13},{13,9},{2,6},{6,2},{1... | collective-permute-start | bytes 393224 | tf_op jit(solution)/shard_map/ppermute | solution.py:389
  38.2 8.5 %collective-permute-start.4 = (bf16[32,2048]{1,0:T(8,128)(2,1)S(1)}, bf16[32,2048]{1,0:T(8,128)(2,1)S(1)}, u32[]{:S(2)}, u32[]{:S(2)}) collective-permute-start(bf16[32,2048]{1,0:T(8,128)(2,1)S(1)} %shard_map.83.refs_1_), channel_id=1, source_target_pairs={{0,12},{4,8},{8,4},{12,0},{1,13},{5,9},{9,5},{13,1},{2,14},{6,10},... | collective-permute-start | bytes 393224 | tf_op jit(solution)/shard_map/ppermute | solution.py:389
  47.4 1.6 %collective-permute-start.10 = (bf16[2,64,1024]{2,1,0:T(8,128)(2,1)S(1)}, bf16[2,64,1024]{2,1,0:T(8,128)(2,1)S(1)}, u32[]{:S(2)}, u32[]{:S(2)}) collective-permute-start(bf16[2,64,1024]{2,1,0:T(8,128)(2,1)S(1)} %get-tuple-element.42), channel_id=1, source_target_pairs={{0,1},{1,0},{2,3},{3,2},{4,5},{5,4},{6,7},{7,6},{8,9},{9,8},{10,11... | collective-permute-start | bytes 786440 | tf_op jit(solution)/shard_map/ppermute | solution.py:423
  49.1 7.3 %collective-permute-start.12 = (bf16[64,1024]{1,0:T(8,128)(2,1)S(1)}, bf16[64,1024]{1,0:T(8,128)(2,1)S(1)}, u32[]{:S(2)}, u32[]{:S(2)}) collective-permute-start(bf16[64,1024]{1,0:T(8,128)(2,1)S(1)} %get-tuple-element.43), channel_id=1, source_target_pairs={{0,8},{1,0},{2,12},{3,4},{4,9},{5,1},{6,13},{7,5},{8,10},{9,2},{10... | collective-permute-start | bytes 393224 | tf_op jit(solution)/shard_map/ppermute | solution.py:431
  52.3 6.7 %collective-permute-start.11 = (bf16[64,1024]{1,0:T(8,128)(2,1)S(1)}, bf16[64,1024]{1,0:T(8,128)(2,1)S(1)}, u32[]{:S(2)}, u32[]{:S(2)}) collective-permute-start(bf16[64,1024]{1,0:T(8,128)(2,1)S(1)} %get-tuple-element.44), channel_id=1, source_target_pairs={{0,12},{1,4},{2,8},{3,0},{4,13},{5,5},{6,9},{7,1},{8,14},{9,6},{10... | collective-permute-start | bytes 393224 | tf_op jit(solution)/shard_map/ppermute | solution.py:431
